TPU v7x, 256 devices: a whole 4x4x8 slice. The times are simulated.
256 devices in a mesh: dp: 32 (over z, x_hi, core), row: 4 (over y), col: 2 (over x_lo).
Axes of the slice: x: 4 (x_hi: 2, x_lo: 2; x = x_hi * 2 + x_lo), y: 4, z: 8, core: 2. Of those that a mesh axis runs over, the one named last changes fastest.
Arguments:
- tokens: bfloat16 [6144, 4096], P('dp', ('row', 'col')), may hold values from -6 to 6
- in_weight: bfloat16 [4096, 3, 4096], P('dp', None, ('row', 'col')), may hold values from -0.09375 to 0.09375
- short_filter: float32 [3, 3, 4096], P(None, None, ('row', 'col')), may hold values from -3 to 3
- long_filter: bfloat16 [256, 128], P(('row', 'col')), may hold values from -0.59765625 to 0.59765625
- grad_out: bfloat16 [6144, 4096], P('dp', ('row', 'col')), may hold values from -6 to 6
Outputs:
- mixed: bfloat16 [6144, 4096], P('dp', ('row', 'col'))
- grad_in: bfloat16 [6144, 4096], P('dp', ('row', 'col'))
- grad_weight: float32 [4096, 3, 4096], P('dp', None, ('row', 'col'))
- grad_long: float32 [256, 128], P(('row', 'col'))
- grad_short: float32 [3, 3, 4096], P(None, None, ('row', 'col'))
All inputs are finite; a program needn't handle non-finite values.
Results may differ from a plain program's by a relative error of at most 0.019.
Values may be sent and summed in bfloat16 or wider, within the bound.
A program may use at most 128 MiB of HBM per device.

v0:
```python
import jax
import jax.numpy as jnp
from jax import lax
from jax.sharding import PartitionSpec as P


def from_behind(block, axis, distance):
    devices = range(lax.axis_size(axis))
    route = [(i - distance, i) for i in devices if i - distance in devices]
    return lax.ppermute(block, axis, route)


def toeplitz(leading, rows, span):
    groups = leading.shape[0]
    width = rows + span
    seed_row = jnp.concatenate(
        [leading, jnp.zeros((groups, width - leading.shape[1]), leading.dtype)], axis=1
    )
    tiled = jnp.tile(seed_row, (1, rows))
    skewed = tiled[:, : rows * (width - 1)].reshape(groups, rows, width - 1)
    return skewed[:, :, :span]


def to_groups(values, ngroups, members):
    count = values.shape[0]
    return values.reshape(count, ngroups, members).transpose(1, 2, 0)


def from_groups(values):
    groups, members, count = values.shape
    return values.transpose(2, 0, 1).reshape(count, groups * members)


def per_device(tokens, in_weight, short_filter, long_filter, grad_out):
    rows = tokens.shape[0]
    local = grad_out.shape[1]
    nshort = short_filter.shape[0]
    ntaps = long_filter.shape[1]
    ngroups = long_filter.shape[0]
    members = local // ngroups
    margin = ntaps - 1
    span = rows + margin
    scale = float(rows * lax.axis_size("dp")) ** (-0.5)
    whole = lax.all_gather(tokens, ("row", "col"), axis=1, tiled=True)
    full_w = lax.all_gather(in_weight, "dp", axis=0, tiled=True)
    mixed_in = jnp.einsum("sd,dic->sic", whole, full_w, preferred_element_type=jnp.float32).astype(
        jnp.bfloat16
    )
    before = from_behind(mixed_in[rows - margin - nshort + 1 :], "dp", 1)
    extended = jnp.concatenate([before, mixed_in], axis=0).astype(jnp.float32)
    long_feats = jnp.zeros((span, 3, local), jnp.float32)
    for j in range(nshort):
        long_feats = (
            long_feats + short_filter[j][None] * extended[nshort - 1 - j : nshort - 1 - j + span]
        )
    product_ext = (long_feats[:, 1] * long_feats[:, 2]).astype(jnp.bfloat16)
    feats = long_feats[margin:]
    short_rows = extended[margin:]
    product_cols = to_groups(product_ext, ngroups, members)
    causal = toeplitz(long_filter[:, ::-1], rows, span)
    conv = from_groups(
        jnp.einsum("gst,gct->gcs", causal, product_cols, preferred_element_type=jnp.float32)
    )
    mixed = (feats[:, 0] * conv).astype(jnp.bfloat16)
    upstream = grad_out.astype(jnp.float32)
    grad_query = upstream * conv
    grad_conv = (upstream * feats[:, 0]).astype(jnp.bfloat16)
    after = from_behind(grad_conv[:margin], "dp", -1)
    grad_ext = jnp.concatenate([grad_conv, after], axis=0)
    anti = toeplitz(long_filter, rows, span)
    grad_product = from_groups(
        jnp.einsum(
            "gst,gct->gcs",
            anti,
            to_groups(grad_ext, ngroups, members),
            preferred_element_type=jnp.float32,
        )
    )
    reversed_cols = jnp.concatenate(
        [product_cols[:, :, ::-1], jnp.zeros((ngroups, members, rows), product_cols.dtype)], axis=2
    )
    width = span + rows
    pairs = jnp.einsum(
        "gcs,gcu->gsu",
        to_groups(grad_conv, ngroups, members),
        reversed_cols,
        preferred_element_type=jnp.float32,
    )
    diagonal = pairs.reshape(ngroups, rows * width)[:, : rows * (width - 1)].reshape(
        ngroups, rows, width - 1
    )
    filter_part = jnp.sum(diagonal[:, :, rows - 1 : rows - 1 + ntaps], axis=1)
    grad_feats = jnp.stack(
        [grad_query, grad_product * feats[:, 2], grad_product * feats[:, 1]], axis=1
    )
    later = from_behind(grad_feats[: nshort - 1], "dp", -1)
    feats_ext = jnp.concatenate([grad_feats, later], axis=0)
    grad_acc = jnp.zeros((rows, 3, local), jnp.float32)
    for j in range(nshort):
        grad_acc = grad_acc + short_filter[j][None] * feats_ext[j : j + rows]
    grad_mixed = grad_acc.astype(jnp.bfloat16)
    short_part = jnp.stack(
        [
            jnp.sum(grad_feats * short_rows[nshort - 1 - j : nshort - 1 - j + rows], axis=0)
            for j in range(nshort)
        ]
    )
    filter_total, short_total = (
        lax.psum(filter_part.astype(jnp.bfloat16), "dp").astype(jnp.float32),
        lax.psum(short_part.astype(jnp.bfloat16), "dp").astype(jnp.float32),
    )
    grad_long = filter_total * scale
    grad_short = short_total * scale
    partial_in = jnp.einsum("sic,dic->sd", grad_mixed, full_w, preferred_element_type=jnp.float32)
    summed_in = lax.psum_scatter(
        partial_in.astype(jnp.bfloat16), ("row", "col"), scatter_dimension=1, tiled=True
    )
    weight_term = (
        jnp.einsum("sd,sic->dic", whole, grad_mixed, preferred_element_type=jnp.float32) * scale
    )
    grad_weight = lax.psum_scatter(
        weight_term.astype(jnp.bfloat16), "dp", scatter_dimension=0, tiled=True
    ).astype(jnp.float32)
    return (mixed, summed_in, grad_weight, grad_long, grad_short)


def solution(mesh):
    placed = (
        P("dp", ("row", "col")),
        P("dp", None, ("row", "col")),
        P(None, None, ("row", "col")),
        P(("row", "col"), None),
        P("dp", ("row", "col")),
    )
    return jax.shard_map(
        per_device,
        mesh=mesh,
        in_specs=placed,
        out_specs=(
            P("dp", ("row", "col")),
            P("dp", ("row", "col")),
            P("dp", None, ("row", "col")),
            P(("row", "col"), None),
            P(None, None, ("row", "col")),
        ),
        check_vma=False,
    )
```

profile of v0, /device:TPU:1, one launch (start us, length us, event | category | flops | bytes accessed | tf_op | source)
XLA Modules:
  0.0 537.0 jit_solution(406576866576352220)
XLA Ops:
  7.2 0.7 all-gather.3.cloned.1.call-update
  7.9 0.7 all-gather.5.cloned.1.call-update
  8.7 49.2 %all-gather.3.cloned.1.call-done = bf16[192,4096]{1,0:T(8,128)(2,1)} async-done(((bf16[192,512]{1,0:T(8,128)(2,1)}), bf16[192,4096]{1,0:T(8,128)(2,1)}) %all-gather.3.cloned.1.call-update) | async-done | bytes 1572880 | tf_op jit(solution)/shard_map/all_gather | solution.py:44
  57.9 120.4 %all-gather.5.cloned.1.call-done = bf16[4096,3,512]{2,0,1:T(8,128)(2,1)} async-done(((bf16[128,3,512]{2,0,1:T(8,128)(2,1)}), bf16[4096,3,512]{2,0,1:T(8,128)(2,1)}) %all-gather.5.cloned.1.call-update) | async-done | bytes 12582928 | tf_op jit(solution)/shard_map/all_gather | solution.py:45
  178.3 7.7 %fusion.10 = bf16[192,3,512]{2,0,1:T(8,128)(2,1)S(1)} fusion(bf16[4096,3,512]{2,0,1:T(8,128)(2,1)} %all-gather.5.cloned.1.call-done, bf16[192,4096]{1,0:T(8,128)(2,1)} %all-gather.3.cloned.1.call-done), kind=kOutput, calls=%fused_computation.16 | convolution fusion | flops 2416214016 | bytes 14745600 | tf_op jit(solution)/shard_map/sd,dic->sic/dot_general | solution.py:46
  186.1 2.3 collective-permute-start
  188.5 3.1 tile.8
  191.7 11.6 %tile.9 = bf16[32,98112]{1,0:T(8,128)(2,1)} reshape(bf16[32,192,511]{2,1,0:T(8,128)(2,1)} %tile.8) | data formatting | bytes 12558336 | tf_op jit(solution)/shard_map/tile | solution.py:19
  203.3 5.8 %slice.119 = bf16[32,97920]{1,0:T(8,128)(2,1)} slice(bf16[32,98112]{1,0:T(8,128)(2,1)} %tile.9), slice={[0:32], [0:97920]} | slice | bytes 12533760 | tf_op jit(solution)/shard_map/slice | solution.py:20
  209.1 15.3 %reshape.49 = bf16[32,192,510]{2,1,0:T(8,128)(2,1)} reshape(bf16[32,97920]{1,0:T(8,128)(2,1)} %slice.119) | data formatting | bytes 12533760 | tf_op jit(solution)/shard_map/reshape | solution.py:20
  224.5 0.3 maximum_convert_fusion
  224.7 0.6 fusion.5
  225.3 1.3 copy-done
  226.7 0.2 copy.24
  226.9 4.1 fusion.3
  231.0 0.9 copy.25
  232.0 1.9 fusion.23
  233.9 2.2 collective-permute-start.1
  236.1 3.2 tile.20
  239.3 11.6 %tile.21 = bf16[32,98112]{1,0:T(8,128)(2,1)} reshape(bf16[32,192,511]{2,1,0:T(8,128)(2,1)} %tile.20) | data formatting | bytes 12558336 | tf_op jit(solution)/shard_map/tile | solution.py:19
  250.9 5.8 %slice.122 = bf16[32,97920]{1,0:T(8,128)(2,1)} slice(bf16[32,98112]{1,0:T(8,128)(2,1)} %tile.21), slice={[0:32], [0:97920]} | slice | bytes 12533760 | tf_op jit(solution)/shard_map/slice | solution.py:20
  256.8 15.3 %reshape.52 = bf16[32,192,510]{2,1,0:T(8,128)(2,1)} reshape(bf16[32,97920]{1,0:T(8,128)(2,1)} %slice.122) | data formatting | bytes 12533760 | tf_op jit(solution)/shard_map/reshape | solution.py:20
  272.1 0.9 copy.27
  273.0 4.2 fusion.1
  277.2 0.9 copy.28
  278.2 1.4 slice_multiply_fusion.10
  279.6 1.9 collective-permute-start.2
  281.6 4.6 collective-permute-done.2
  286.3 0.8 fusion.15
  287.1 0.6 copy-done.6
  287.7 6.6 %multiply_convert_fusion = bf16[3,512,4096]{2,1,0:T(8,128)(2,1)} fusion(bf16[192,3,512]{2,0,1:T(8,128)(2,1)S(1)} %get-tuple-element.29, bf16[192,4096]{1,0:T(8,128)(2,1)S(1)} %copy-done.6), kind=kOutput, calls=%fused_computation | convolution fusion | flops 2428502016 | bytes 14745600 | tf_op jit(solution)/shard_map/sd,sic->dic/dot_general | solution.py:119
  294.3 16.6 %copy.34 = bf16[4096,1536]{1,0:T(8,128)(2,1)} copy(bf16[4096,1536]{0,1:T(8,128)(2,1)} %bitcast.62) | data formatting | bytes 25165824
  311.0 0.3 reduce-scatter.5.cloned.1.call-start
  311.2 0.8 copy-done.2
  312.0 10.0 %fusion = bf16[192,4096]{1,0:T(8,128)(2,1)} fusion(bf16[192,3,512]{2,0,1:T(8,128)(2,1)S(1)} %copy-done.2, bf16[4096,3,512]{2,0,1:T(8,128)(2,1)} %all-gather.5.cloned.1.call-done), kind=kOutput, calls=%fused_computation.2 | convolution fusion | flops 2416705536 | bytes 14745600 | tf_op jit(solution)/shard_map/sic,dic->sd/dot_general | solution.py:114
  322.2 0.5 reverse
  322.7 0.2 slice.183
  322.8 7.0 %fusion.20 = f32[32,192,511]{2,1,0:T(8,128)} fusion(bf16[32,16,192]{2,1,0:T(8,128)(2,1)S(1)} %bitcast.69, bf16[32,16,319]{2,1,0:T(8,128)(2,1)S(1)} %slice.183), kind=kOutput, calls=%fused_computation.33 | convolution fusion | flops 100466688 | bytes 13081600 | tf_op jit(solution)/shard_map/gcs,gcu->gsu/dot_general | solution.py:83
  329.8 13.1 %reshape.55 = f32[32,98112]{1,0:T(8,128)} reshape(f32[32,192,511]{2,1,0:T(8,128)} %fusion.20) | data formatting | bytes 25116672 | tf_op jit(solution)/shard_map/reshape | solution.py:89
  343.0 11.4 %slice.129 = f32[32,97920]{1,0:T(8,128)} slice(f32[32,98112]{1,0:T(8,128)} %reshape.55), slice={[0:32], [0:97920]} | slice | bytes 25067520 | tf_op jit(solution)/shard_map/slice | solution.py:89
  354.4 15.1 %reshape.56 = f32[32,192,510]{2,1,0:T(8,128)} reshape(f32[32,97920]{1,0:T(8,128)} %slice.129) | data formatting | bytes 25067520 | tf_op jit(solution)/shard_map/reshape | solution.py:89
  369.5 3.7 slice_reduce_fusion
  373.2 124.9 %all-reduce.3 = (bf16[32,128]{1,0:T(8,128)(2,1)S(1)}, bf16[3,3,512]{2,1,0:T(4,128)(2,1)S(1)}) all-reduce(bf16[32,128]{1,0:T(8,128)(2,1)S(1)} %slice_reduce_fusion, bf16[3,3,512]{2,1,0:T(4,128)(2,1)S(1)} %pad_maximum_fusion.3), channel_id=1, replica_groups=mesh['dp'=32,'row'=4,'col'=2] {'dp'}, use_global_device_ids=true, to_apply=%region_3.0 | all-reduce | flops 8704 | bytes 34816 | tf_op jit(solution)/shard_map/psum | solution.py:109
  498.1 0.6 convert_multiply_fusion.3
  498.7 0.6 convert_multiply_fusion.2
  499.3 1.2 copy.35
  500.6 1.1 copy.31
  501.6 28.9 %reduce-scatter.5.cloned.1.call-done = bf16[192,512]{1,0:T(8,128)(2,1)} async-done(((bf16[192,4096]{1,0:T(8,128)(2,1)}), bf16[192,512]{1,0:T(8,128)(2,1)}) %reduce-scatter.5.cloned.1.call-update) | async-done | bytes 196624 | tf_op jit(solution)/shard_map/reduce_scatter | solution.py:115
  (32 shorter events, 0.9 us)
Async XLA Ops:
  7.2 50.7 %all-gather.3.cloned.1.call-start = ((), (), s32[]{:S(2)}) async-start(), calls=%async_computation.2 | async-start | bytes 1769472 | tf_op jit(solution)/shard_map/all_gather | solution.py:44
  7.9 170.4 %all-gather.5.cloned.1.call-start = ((), (), s32[]{:S(2)}) async-start(), calls=%async_computation.3 | async-start | bytes 12976128 | tf_op jit(solution)/shard_map/all_gather | solution.py:45
  8.6 179.8 %copy-start.4 = (bf16[32,128]{1,0:T(8,128)(2,1)S(1)}, bf16[32,128]{1,0:T(8,128)(2,1)}, u32[]{:S(2)}) copy-start(bf16[32,128]{1,0:T(8,128)(2,1)} %param.8) | copy-start | bytes 24580
  8.7 490.7 %reduce-scatter.7.cloned.1.call-start = ((), (), s32[]{:S(2)}) async-start(), calls=%async_computation.5 | async-start | bytes 12976128
  186.1 38.4 %collective-permute-start = (bf16[129,3,512]{2,0,1:T(8,128)(2,1)S(1)}, bf16[129,3,512]{2,0,1:T(8,128)(2,1)S(1)}, u32[]{:S(2)}, u32[]{:S(2)}) collective-permute-start(bf16[129,3,512]{2,0,1:T(8,128)(2,1)S(1)} %slice.112), channel_id=1, source_target_pairs={{0,8},{8,16},{16,24},{24,32},{32,40},{40,48},{48,56},{56,64},{64,7... | collective-permute-start | bytes 1188872 | tf_op jit(solution)/shard_map/ppermute | solution.py:10
  209.1 15.3 %copy-start.5 = (f32[3,3,512]{2,1,0:T(4,128)S(1)}, f32[3,3,512]{2,1,0:T(4,128)}, u32[]{:S(2)}) copy-start(f32[3,3,512]{2,1,0:T(4,128)} %param.7) | copy-start | bytes 55300
  225.3 1.3 copy-start
  226.9 5.1 copy-start.3
  233.9 38.2 %collective-permute-start.1 = (bf16[127,512]{1,0:T(8,128)(2,1)S(1)}, bf16[127,512]{1,0:T(8,128)(2,1)S(1)}, u32[]{:S(2)}, u32[]{:S(2)}) collective-permute-start(bf16[127,512]{1,0:T(8,128)(2,1)S(1)} %slice.121), channel_id=1, source_target_pairs={{8,0},{16,8},{24,16},{32,24},{40,32},{48,40},{56,48},{64,56},{72,6... | collective-permute-start | bytes 390152 | tf_op jit(solution)/shard_map/ppermute | solution.py:10
  279.6 6.5 %collective-permute-start.2 = (f32[2,3,512]{2,0,1:T(2,128)S(1)}, f32[2,3,512]{2,0,1:T(2,128)S(1)}, u32[]{:S(2)}, u32[]{:S(2)}) collective-permute-start(f32[2,3,512]{2,0,1:T(2,128)S(1)} %slice.126), channel_id=1, source_target_pairs={{8,0},{16,8},{24,16},{32,24},{40,32},{48,40},{56,48},{64,56},{72,6... | collective-permute-start | bytes 36872 | tf_op jit(solution)/shard_map/ppermute | solution.py:10
  286.3 1.4 copy-start.6
  287.1 7.2 %copy-start.1 = (bf16[192,3,512]{2,0,1:T(8,128)(2,1)}, bf16[192,3,512]{2,0,1:T(8,128)(2,1)S(1)}, u32[]{:S(2)}) copy-start(bf16[192,3,512]{2,0,1:T(8,128)(2,1)S(1)} %get-tuple-element.29) | copy-start | bytes 1769476
  310.9 1.1 copy-start.2
  311.0 219.5 %reduce-scatter.5.cloned.1.call-start = ((), (), s32[]{:S(2)}) async-start(), calls=%async_computation.4 | async-start | bytes 1769472 | tf_op jit(solution)/shard_map/reduce_scatter | solution.py:115
Sparse Core Ops, SparseCore 0:
  9.8 48.0 all-gather.2
  60.7 117.5 all-gather.4
  311.1 170.3 reduce-scatter.6
  484.5 45.9 reduce-scatter.4
where the time goes:
time: 540 us; the launch traced here: 537 us
  waiting for transfers between devices  204 us (38%)
  local copies, waits for them, and re-layouts  137 us (25%)
  blocking collectives  125 us (23%)
  matrix products  39.5 us (7%)
  between operations  14 us (3%)
  other arithmetic  10.2 us (2%)
  starting transfers between devices  6.82 us (1%)
    psum x1, blocking collectives, per_device(): lax.psum(filter_part.astype(jnp.bfloat16), 'dp').astype(jnp.float32)  125 us
    all_gather x1, waiting for transfers between devices, per_device(): full_w = lax.all_gather(in_weight, 'dp', axis=0, tiled=True)  120 us
    all_gather x1, waiting for transfers between devices, per_device(): whole = lax.all_gather(tokens, ('row', 'col'), axis=1, tiled=True)  49.2 us
    reshape x2, local copies, waits for them, and re-layouts, toeplitz(): skewed = tiled[:, :rows * (width - 1)].reshape(groups, rows, width - 1)  30.6 us
    another operation x4, local copies, waits for them, and re-layouts, toeplitz(): tiled = jnp.tile(seed_row, (1, rows))  29.5 us
    reduce_scatter x1, waiting for transfers between devices, per_device(): lax.psum_scatter(partial_in.astype(jnp.bfloat16), ('row', 'col'), scatter...  28.9 us
    reshape x2, local copies, waits for them, and re-layouts, per_device(): pairs.reshape(ngroups, rows * width)[:, :rows * (width - 1)]  28.3 us
    unnamed x19, local copies, waits for them, and re-layouts  22.2 us
  transfers between devices with their start and end apart: 7, of which 4 were waited for; matrix products, arithmetic and copies ran while one was open for 25% of the time, Pallas kernels for 0%

commit v1 on v0

v1 whole, which is shorter than its diff:
```python
import jax
import jax.numpy as jnp
from jax import lax
from jax.experimental import pallas as pl
from jax.experimental.pallas import tpu as pltpu
from jax.sharding import PartitionSpec as P

MESH = pl.DeviceIdType.MESH
F32, BF16 = jnp.float32, jnp.bfloat16
SIGNS = (1, -1)
LINK_RATE = {"z": 46.0e3, "x": 46.0e3, "y": 46.0e3, "d": 200.0e3}
LINK_LATENCY = {"z": 1.6, "x": 1.6, "y": 1.6, "d": 1.0}


def planned_order(tasks, msgs):
    arrival, done, link_free = {}, {}, {}
    left, order, now = list(tasks), [], 0.0
    while left:
        best = None
        for at, task in enumerate(left):
            ready = 0.0
            for dep in task["deps"]:
                when = arrival.get(dep, done.get(dep))
                if when is None:
                    ready = None
                    break
                ready = max(ready, when)
            if ready is None:
                continue
            key = (max(ready, now), task["prio"], ready, at)
            if best is None or key < best[0]:
                best = (key, at)
        task = left.pop(best[1])
        now = best[0][0] + task["cost"]
        done[task["name"]] = now
        order.append(task)
        for name in task["sends"]:
            link, nbytes, hops = msgs[name]["link"], msgs[name]["bytes"], msgs[name]["hops"]
            begin = max(now, link_free.get(link, 0.0))
            link_free[link] = begin + nbytes * hops / LINK_RATE[link[0]]
            arrival[name] = link_free[link] + LINK_LATENCY[link[0]] * hops
    return order, now


def block_kernel(
    tokens, w3, sf, lf, gout, mixed_out, gin_out, gw_out, gl_out, gs_out,
    tok, wst, wb, go, acc, mx, gox, toe, voe, lfs, sfs, mxo, mxt, mr, gmt, gm,
    glb, gsb, smv, smr, smt, sqr, gp, ws, wr, fs, fr, pp, pr, q1, h1s, h1, s1, q2, h2s, h2,
    ssem, rsem, *, nz, scale,
):
    dp, y, xl = lax.axis_index("dp"), lax.axis_index("row"), lax.axis_index("col")
    z, r = dp // 4, dp % 4
    xh, c = r // 2, r % 2
    x = xh * 2 + xl
    rows, cols = tokens.shape
    quarter = rows // 4
    ntok = 4 * rows
    ngroups, members = mx.shape[1], mx.shape[2]
    nblocks = ntok // 128
    half_z = nz // 2

    def wrap(value, n):
        return lax.rem(value + 2 * n, n)

    def mate(m):
        other_h = 1 - xh if m & 2 else xh
        other_c = 1 - c if m & 1 else c
        return other_h * 2 + other_c

    def at_z(e):
        return (wrap(z + e, nz) * 4 + r, y, xl)

    def at_quad(m):
        return (z * 4 + mate(m), y, xl)

    def at_xy(axis, d):
        if axis == "y":
            return (dp, wrap(y + d, 4), xl)
        there = wrap(x + d, 4)
        return (z * 4 + (there // 2) * 2 + c, y, there % 2)

    def place(axis, first, second):
        dx, dy = (first, second) if axis == "x" else (second, first)
        px, py = wrap(x + dx, 4), wrap(y + dy, 4)
        return py * 2 + px % 2, px // 2

    msgs, tasks = {}, []

    def msg(name, src, dst, dev, link, nbytes, hops=1):
        msgs[name] = dict(src=src, dst=dst, dev=dev, link=link, bytes=nbytes, hops=hops, index=len(msgs))
        return name

    def task(name, deps=(), run=None, sends=(), cost=0.02, prio=5):
        tasks.append(dict(name=name, deps=list(deps), run=run, sends=list(sends), cost=cost, prio=prio))
        return name

    def copy_of(name):
        m = msgs[name]
        i = m["index"]
        return pltpu.make_async_remote_copy(
            src_ref=m["src"](), dst_ref=m["dst"](), send_sem=ssem.at[i], recv_sem=rsem.at[i],
            device_id=m["dev"](), device_id_type=MESH,
        )

    def lanes(block):
        return pl.ds(pl.multiple_of(block * 128, 128), 128)

    wbytes = 128 * 384 * 2
    for m in (1, 2, 3):
        link, hops = ("d", 1) if m == 1 else ("x+", 2)
        msg(("wq", m), lambda m=m: wst.at[mate(m)], lambda: wb.at[z, r], lambda m=m: at_quad(m), link, wbytes, hops)
        msg(("goq", m), lambda m=m: gout.at[:, lanes(mate(m))], lambda: go.at[r], lambda m=m: at_quad(m), link, rows * 256, hops)
    task("quad_w", sends=[("wq", 1), ("wq", 2), ("wq", 3)], prio=0)
    task("quad_go", deps=["quad_w", "tok_first"], sends=[("goq", 1), ("goq", 2), ("goq", 3)], prio=1)

    def reach(m, d, gather):
        return half_z if (m < 2) == (d > 0) else half_z - 1

    for m in range(4):
        for d in SIGNS:
            for h in range(1, reach(m, d, True) + 1):
                where = lambda m=m, d=d, h=h: wb.at[wrap(z - d * (h - 1), nz), mate(m)]
                name = msg(("w", m, d, h), where, where, lambda d=d: at_z(d), "z+" if d > 0 else "z-", wbytes)
                if h > 1:
                    deps = [("w", m, d, h - 1)]
                else:
                    deps = [("wq", m)] if m else []
                task(("send", name), deps=deps, sends=[name], prio=0 if m < 2 else 1)

    hb, qb = 2 * quarter * cols * 2, quarter * cols * 2
    token_msgs = []
    for h in (0, 1):
        a1, a2 = ("x", "y") if h == 0 else ("y", "x")

        def piece(o, u, part, h=h, a1=a1):
            k, ph = place(a1, o, u)
            begin, size = {0: (0, 2), 1: (0, 1), -1: (1, 1)}[part]
            return tok.at[k, ph * 2 + c, pl.ds(h * 2 * quarter + begin * quarter, size * quarter), :]

        for d in SIGNS:
            w = lambda piece=piece: piece(0, 0, 0)
            msg(("t1", h, d), w, w, lambda a1=a1, d=d: at_xy(a1, d), a1 + "+-"[d < 0], hb)
            w = lambda piece=piece, d=d: piece(-d, 0, d)
            msg(("t1q", h, d), w, w, lambda a1=a1, d=d: at_xy(a1, d), a1 + "+-"[d < 0], qb)
            for o in (0, -1, 1, 2):
                w = lambda piece=piece, o=o: piece(o, 0, 0)
                msg(("t2", h, o, d), w, w, lambda a2=a2, d=d: at_xy(a2, d), a2 + "+-"[d < 0], hb)
                w = lambda piece=piece, o=o, d=d: piece(o, -d, d)
                msg(("t2q", h, o, d), w, w, lambda a2=a2, d=d: at_xy(a2, d), a2 + "+-"[d < 0], qb)
                token_msgs += [("t2", h, o, d), ("t2q", h, o, d)]
            token_msgs += [("t1", h, d), ("t1q", h, d)]
        for o in (0, -1, 1, 2):
            for u in (0, -1, 1, 2):
                w = lambda piece=piece, o=o, u=u: piece(o, u, 0)
                msg(("td", h, o, u), w, w, lambda: at_quad(1), "d", hb)
                token_msgs.append(("td", h, o, u))
        have = {0: [], -1: [("t1", h, 1)], 1: [("t1", h, -1)], 2: [("t1q", h, 1), ("t1q", h, -1)]}
        task(("tok1", h), deps=[], sends=[("t1", h, 1), ("t1", h, -1)], prio=0)
        for d in SIGNS:
            task(("tok1q", h, d), deps=[("t1", h, d)], sends=[("t1q", h, d)], prio=1)
        for o in (0, -1, 1, 2):
            task(("tok2", h, o), deps=have[o] + [("tok1", h)], sends=[("t2", h, o, 1), ("t2", h, o, -1)], prio=2)
            for d in SIGNS:
                task(("tok2q", h, o, d), deps=[("t2", h, o, d)], sends=[("t2q", h, o, d)], prio=2)
            there = {0: have[o], -1: [("t2", h, o, 1)], 1: [("t2", h, o, -1)], 2: [("t2q", h, o, 1), ("t2q", h, o, -1)]}
            for u in (0, -1, 1, 2):
                task(("tokd", h, o, u), deps=there[u], sends=[("td", h, o, u)], prio=3)
    task("tok_first", deps=[("tok1", 0), ("tok1", 1)], prio=0)
    task("tok_all", deps=token_msgs, prio=4)

    def first_matmul(e, far):
        zs = wrap(z - e, nz)
        hf = 1 - xh if far else xh

        def tile(rr, carry):
            lhs = tok[zs, rr, :, pl.ds(pl.multiple_of(hf * 256, 256), 256)]
            rhs = wb[zs, pl.ds(hf * 2, 2)].reshape(256, 384)
            acc[rr] += jnp.dot(lhs, rhs, preferred_element_type=F32)
            return carry

        lax.fori_loop(0, 4, tile, 0)

    mm = []
    for far in (False, True):
        for e in range(-half_z + 1, half_z + 1):
            pair = (2, 3) if far else (0, 1)
            if e == 0:
                deps = [("wq", m) for m in pair if m]
            elif e == half_z:
                d = -1 if far else 1
                deps = [("w", m, d, half_z) for m in pair]
            else:
                deps = [("w", m, 1 if e > 0 else -1, abs(e)) for m in pair]
            mm.append(task(("mm", e, far), deps=["tok_all"] + deps, run=lambda e=e, far=far: first_matmul(e, far), cost=0.55, prio=6))

    def build_toeplitz():
        for q in range(4):
            lfs[q] = lf[q * ngroups : (q + 1) * ngroups, :].astype(F32)
        for j in range(3):
            sfs[3 * j : 3 * j + 3, :] = sf[j, :, lanes(r)]

        def one(g, carry):
            row = lfs[r, pl.ds(g, 1), :]
            line = jnp.concatenate([row, jnp.zeros_like(row)], axis=1)
            skew = pltpu.roll(jnp.broadcast_to(line, (256, 256)), 0, 1, stride=1, stride_axis=0).astype(BF16)
            toe[g, 0:128, :] = skew[128:256, 0:128]
            toe[g, 128:256, :] = skew[0:128, 0:128]
            voe[g] = skew[0:128, :]
            return carry

        lax.fori_loop(0, ngroups, one, 0)
        sfs[...] = sfs[...].T

    task("toe", run=build_toeplitz, cost=3.0, prio=8)

    def turn_gout():
        flat = go[...].reshape(ntok, 128).T
        gox[:, :, 0:ntok] = flat.reshape(ngroups, members, ntok)

    msg("goh", lambda: gox.at[:, :, pl.ds(0, 256)], lambda: gox.at[:, :, pl.ds(ntok, 256)], lambda: at_z(-1), "z-", 128 * 512)
    task("got", deps=[("goq", 1), ("goq", 2), ("goq", 3)], run=turn_gout, sends=["goh"], cost=0.6, prio=7)

    def turn_mixed():
        for i in range(3):
            flat = acc[:, :, i * 128 : (i + 1) * 128].reshape(ntok, 128).astype(BF16).T
            mx[i, :, :, 256 : 256 + ntok] = flat.reshape(ngroups, members, ntok)

    msg(("mh", 1), lambda: mx.at[:, :, :, pl.ds(ntok, 256)], lambda: mx.at[:, :, :, pl.ds(0, 256)], lambda: at_z(1), "z+", 384 * 512)
    msg(("mh", -1), lambda: mx.at[:, :, :, pl.ds(256, 256)], lambda: mx.at[:, :, :, pl.ds(256 + ntok, 256)], lambda: at_z(-1), "z-", 384 * 512)
    task("mxt", deps=mm, run=turn_mixed, sends=[("mh", 1), ("mh", -1)], cost=1.5, prio=0)

    span = ntok + 128

    def local_operator():
        lane = lax.broadcasted_iota(jnp.int32, (members, 128), 1)
        flip = (
            lax.broadcasted_iota(jnp.int32, (128, 128), 0) + lax.broadcasted_iota(jnp.int32, (128, 128), 1) == 127
        ).astype(F32).astype(BF16)
        width = ntok + 512
        position = lax.broadcasted_iota(jnp.int32, (members, width), 1)
        low = jnp.where(z == 0, 256, 0)
        high = jnp.where(z == nz - 1, 256 + ntok, width)
        inside = (position >= low) & (position < high)

        def group(g, carry):
            taps = sfs[pl.ds(pl.multiple_of(g * members, members), members), :]

            def tap(j, i):
                return taps[:, 3 * j + i : 3 * j + i + 1]

            lag, feats = [], []
            for i in range(3):
                base = jnp.where(inside, mx[i, g].astype(F32), 0.0)
                lag.append([base, pltpu.roll(base, 1, 1), pltpu.roll(base, 2, 1)])
                feats.append(tap(0, i) * lag[i][0] + tap(1, i) * lag[i][1] + tap(2, i) * lag[i][2])
            product = (feats[1] * feats[2]).astype(BF16)
            windows = jnp.concatenate([product[:, 128 * (b + 1) : 128 * (b + 3)] for b in range(nblocks + 1)], axis=0)
            out = jnp.dot(windows, toe[g], preferred_element_type=F32)
            conv = jnp.concatenate([out[members * b : members * (b + 1)] for b in range(nblocks + 1)], axis=1)
            up = jnp.where(inside[:, 256:], gox[g].astype(F32), 0.0)
            query = feats[0][:, 256:]
            gconv = (up * query).astype(BF16)
            ahead = jnp.concatenate([gconv[:, 128 * b : 128 * (b + 2)] for b in range(nblocks + 1)], axis=0)
            back = lax.dot_general(ahead, voe[g], (((1,), (1,)), ((), ())), preferred_element_type=F32)
            gproduct = jnp.concatenate([back[members * b : members * (b + 1)] for b in range(nblocks + 1)], axis=1)
            mxo[g] = (query[:, :ntok] * conv[:, :ntok]).astype(BF16)
            gfeats = [
                up[:, :span] * conv,
                gproduct * feats[2][:, 256 : 256 + span],
                gproduct * feats[1][:, 256 : 256 + span],
            ]
            sums = jnp.zeros((members, 128), F32)
            for i in range(3):
                grad = tap(0, i) * gfeats[i] + tap(1, i) * pltpu.roll(gfeats[i], span - 1, 1) + tap(2, i) * pltpu.roll(gfeats[i], span - 2, 1)
                gmt[i, g] = grad[:, :ntok].astype(BF16)
                for j in range(3):
                    both = gfeats[i][:, :ntok] * lag[i][j][:, 256 : 256 + ntok]
                    part = both[:, 0:128]
                    for b in range(1, nblocks):
                        part = part + both[:, 128 * b : 128 * (b + 1)]
                    sums = jnp.where(lane == 3 * j + i, jnp.sum(part, axis=1, keepdims=True), sums)
            gsb[pl.ds(pl.multiple_of(g * members, members), members), :] = sums
            held = jnp.concatenate([gconv[:, 128 * b : 128 * (b + 1)] for b in range(nblocks)], axis=0)
            flipped = jnp.dot(held, flip, preferred_element_type=F32).astype(BF16)
            pairs = lax.dot_general(flipped, windows[: members * nblocks], (((0,), (0,)), ((), ())), preferred_element_type=F32)
            skew = pltpu.roll(pairs, 0, 1, stride=1, stride_axis=0)
            glb[pl.ds(g, 1), :] = jnp.sum(skew, axis=0, keepdims=True)[:, 128:]
            return carry

        lax.fori_loop(0, ngroups, group, 0)
        unflipped = jnp.dot(glb[...].astype(BF16), flip, preferred_element_type=F32)
        smv[0:8, :] = unflipped
        smv[8:24, :] = gsb[...].T[0:16, :]

    task("local", deps=[("mh", 1), ("mh", -1), "goh", "toe", "got", "mxt"], run=local_operator, cost=9.0, prio=0)

    for m in (1, 2, 3):
        link, hops = ("d", 1) if m == 1 else ("x-", 2)
        msg(
            ("mq", m), lambda m=m: mxt.at[pl.ds(pl.multiple_of(mate(m) * rows, rows), rows), :], lambda: mr.at[r],
            lambda m=m: at_quad(m), link, rows * 256, hops,
        )
        msg(("sq", m), lambda: smt, lambda m=m: sqr.at[m - 1], lambda m=m: at_quad(m), link, 24 * 512, hops)

    def turn_output():
        for g in range(ngroups):
            mxt[:, g * members : (g + 1) * members] = mxo[g].T

    task("mixed_send", deps=["local"], run=turn_output, sends=[("mq", m) for m in (1, 2, 3)], cost=0.7, prio=3.35)
    offsets = [e for e in range(-half_z + 1, half_z + 1) if e]
    for n, e in enumerate(offsets):
        msg(("sm", e), lambda: smv, lambda n=n: smr.at[n], lambda e=e: at_z(e), "z+" if e > 0 else "z-", 24 * 512, abs(e))
    task("small_send", deps=["local"], sends=[("sm", e) for e in offsets], prio=3.36)

    def small_total():
        total = smv[...]
        for n in range(len(offsets)):
            total = total + smr[n]
        smt[...] = total * scale

    task("small_sum", deps=[("sm", e) for e in offsets] + ["small_send"], run=small_total, sends=[("sq", m) for m in (1, 2, 3)], cost=0.1, prio=7)

    def small_out():
        for m in range(4):
            part = smt[...] if m == 0 else sqr[m - 1]
            q = mate(m)
            gl_out[pl.ds(pl.multiple_of(q * 8, 8), 8), :] = part[0:8]
            for j in range(3):
                gs_out[j, :, lanes(q)] = part[8 + 3 * j : 11 + 3 * j]

    task("small_out", deps=[("sq", m) for m in (1, 2, 3)] + ["small_sum"], run=small_out, cost=0.1, prio=9)

    def mixed_final():
        mixed_out[:, lanes(r)] = mxt[pl.ds(pl.multiple_of(r * rows, rows), rows), :]
        for m in (1, 2, 3):
            mixed_out[:, lanes(mate(m))] = mr[mate(m)]

    task("mixed_out", deps=[("mq", m) for m in (1, 2, 3)] + ["mixed_send"], run=mixed_final, cost=0.1, prio=9)

    def weight_partial(e):
        zc = wrap(z + e, nz)
        lhs = gmt[...].reshape(384, ntok)

        def tile(n, carry):
            rhs = tok[zc, :, :, pl.ds(pl.multiple_of(n * 256, 256), 256)].reshape(ntok, 256)
            out = jnp.dot(lhs, rhs, preferred_element_type=F32)
            gp[e % nz, 2 * n] = out[:, 0:128]
            gp[e % nz, 2 * n + 1] = out[:, 128:256]
            return carry

        lax.fori_loop(0, 2, tile, 0)

    chunks = [half_z]
    for e in range(half_z - 1, 0, -1):
        chunks += [e, -e]
    chunks.append(0)
    for n, e in enumerate(chunks):
        task(("gw", e % nz), deps=["local"], run=lambda e=e: weight_partial(e), cost=1.0, prio=3 + 0.1 * n)
    slot = {}
    for m in range(4):
        for d in SIGNS:
            top = reach(m, d, False) if m < 2 else reach(m, d, False)
            for h in range(top, 0, -1):
                slot[m, d, h] = len(slot)
    for m in (2, 3, 0, 1):
        for d in SIGNS:
            top = reach(m, d, False)
            for h in range(top, 0, -1):
                s = slot[m, d, h]
                name = msg(("wr", m, d, h), lambda s=s: ws.at[s], lambda s=s: wr.at[s], lambda d=d: at_z(d), "z+" if d > 0 else "z-", wbytes)
                deps = [("gw", (d * h) % nz)]
                if h < top:
                    deps.append(("wr", m, d, h + 1))

                def add(m=m, d=d, h=h, s=s, top=top):
                    value = gp[(d * h) % nz, mate(m)]
                    if h < top:
                        value = value + wr[slot[m, d, h + 1]].astype(F32)
                    ws[s] = value.astype(BF16)

                task(("send", "wr", m, d, h), deps=deps, run=add, sends=[name], cost=0.12, prio=0 if m >= 2 else 1)

    def weight_total(m):
        return (gp[0, mate(m)] + wr[slot[m, 1, 1]].astype(F32) + wr[slot[m, -1, 1]].astype(F32)) * scale

    def weight_store(m, value):
        for i in range(3):
            gw_out[i, :, lanes(mate(m))] = value[i * 128 : (i + 1) * 128, :].T

    for m in range(4):
        deps = [("gw", 0), ("wr", m, 1, 1), ("wr", m, -1, 1)]
        if m == 0:
            task("wtot0", deps=deps, run=lambda: weight_store(0, weight_total(0)), cost=0.5, prio=8)
            continue
        link, hops = ("d", 1) if m == 1 else ("x-" if m == 2 else "x+", 2)
        msg(("wf", m), lambda m=m: fs.at[m - 1], lambda m=m: fr.at[m - 1], lambda m=m: at_quad(m), link, wbytes, hops)

        def finish(m=m):
            fs[m - 1] = weight_total(m).astype(BF16)

        task(("wtot", m), deps=deps, run=finish, sends=[("wf", m)], cost=0.2, prio=1)
        task(("wout", m), deps=[("wf", m)], run=lambda m=m: weight_store(m, fr[m - 1].astype(F32)), cost=0.5, prio=8)

    def feature_block(dy, dx):
        return wrap(y + dy, 4) * 2 + wrap(xl + dx, 2)

    def token_partial(dy, dx):
        k = feature_block(dy, dx)
        rhs = wb[k].reshape(512, 384)

        def tile(rr, carry):
            lhs = gm[pl.ds(pl.multiple_of(rr * rows, rows), rows), :]
            pp[k, rr] = lax.dot_general(lhs, rhs, (((1,), (1,)), ((), ())), preferred_element_type=F32).astype(BF16)
            return carry

        lax.fori_loop(0, 4, tile, 0)

    def pair_sum(dy, dx):
        k = feature_block(dy, dx)
        for ph in range(2):
            pp[k, ph * 2 + c] = (pp[k, ph * 2 + c].astype(F32) + pr[k, ph].astype(F32)).astype(BF16)

    def turn_grad():
        for i in range(3):
            gm[:, i * 128 : (i + 1) * 128] = gmt[i].reshape(128, ntok).T

    task("turn_grad", deps=["local"], run=turn_grad, cost=1.0, prio=3.15)
    for n, dy in enumerate((2, 1, -1, 0)):
        for dx in (0, 1):
            both = [
                msg(
                    ("pd", dy, dx, ph), lambda dy=dy, dx=dx, ph=ph: pp.at[feature_block(dy, dx), ph * 2 + (1 - c)],
                    lambda dy=dy, dx=dx, ph=ph: pr.at[feature_block(dy, dx), ph], lambda: at_quad(1), "d", rows * cols * 2,
                )
                for ph in range(2)
            ]
            task(("pk", dy, dx), deps=["turn_grad"], run=lambda dy=dy, dx=dx: token_partial(dy, dx), sends=both, cost=1.1, prio=3.21 + 0.12 * n + 0.06 * dx)
            task(("pa", dy, dx), deps=both + [("pk", dy, dx)], run=lambda dy=dy, dx=dx: pair_sum(dy, dx), cost=0.25, prio=2.5)

    def part_rows(h, part):
        begin, size = {0: (0, 2), 1: (0, 1), -1: (1, 1)}[part]
        return pl.ds(h * 2 * quarter + begin * quarter, size * quarter)

    def own_rows(part):
        return slice(0, quarter) if part > 0 else slice(quarter, 2 * quarter)

    for h in (0, 1):
        a1, a2 = ("y", "x") if h == 0 else ("x", "y")

        def needs(o1, o2, h=h):
            dy, dx = (o1, o2) if h == 0 else (o2, o1)
            dy = {0: 0, 1: 1, -1: -1, 2: 2}[dy]
            return ("pa", dy, dx % 2)

        def held(o1, o2, part, h=h, a1=a1):
            k, ph = place(a1, o1, o2)
            return pp.at[k, ph * 2 + c, part_rows(h, part), :]

        for o in (2, 1, -1, 0):
            oi = o % 4
            for d in SIGNS:
                di = 0 if d > 0 else 1
                link1 = a1 + "+-"[d < 0]
                msg(("s1q", h, o, d), lambda held=held, o=o, d=d: held(2, o, d), lambda h=h, oi=oi, di=di: q1.at[h, oi, di], lambda a1=a1, d=d: at_xy(a1, d), link1, qb)
                msg(("s1h", h, o, d), lambda h=h, oi=oi, di=di: h1s.at[h, oi, di], lambda h=h, oi=oi, di=di: h1.at[h, oi, di], lambda a1=a1, d=d: at_xy(a1, d), link1, hb)
                task(("s1q", h, o, d, "go"), deps=[needs(2, o)], sends=[("s1q", h, o, d)], prio=1)

                def forward(h=h, o=o, oi=oi, d=d, di=di, held=held):
                    own = held(d, o, 0)[...]
                    mine, rest = own_rows(d), own_rows(-d)
                    h1s[h, oi, di, mine, :] = (own[mine].astype(F32) + q1[h, oi, di].astype(F32)).astype(BF16)
                    h1s[h, oi, di, rest, :] = own[rest]

                task(("s1h", h, o, d, "go"), deps=[("s1q", h, o, d), needs(d, o)], run=forward, sends=[("s1h", h, o, d)], cost=0.08, prio=2)

            def settle(h=h, o=o, oi=oi, held=held):
                total = held(0, o, 0)[...].astype(F32) + h1[h, oi, 0].astype(F32) + h1[h, oi, 1].astype(F32)
                s1[h, oi] = total.astype(BF16)

            sends = []
            if o == 2:
                for d in SIGNS:
                    di = 0 if d > 0 else 1
                    part = slice(0, quarter) if d > 0 else slice(quarter, 2 * quarter)
                    begin = 0 if d > 0 else quarter
                    sends.append(
                        msg(("s2q", h, d), lambda h=h, begin=begin: s1.at[h, 2, pl.ds(begin, quarter), :], lambda h=h, di=di: q2.at[h, di], lambda a2=a2, d=d: at_xy(a2, d), a2 + "+-"[d < 0], qb)
                    )
            task(("s1", h, o), deps=[("s1h", h, o, 1), ("s1h", h, o, -1), needs(0, o)], run=settle, sends=sends, cost=0.08, prio=2)
        for d in SIGNS:
            di = 0 if d > 0 else 1
            msg(("s2h", h, d), lambda h=h, di=di: h2s.at[h, di], lambda h=h, di=di: h2.at[h, di], lambda a2=a2, d=d: at_xy(a2, d), a2 + "+-"[d < 0], hb)

            def second(h=h, d=d, di=di):
                own = s1[h, d % 4]
                mine, rest = own_rows(d), own_rows(-d)
                h2s[h, di, mine, :] = (own[mine].astype(F32) + q2[h, di].astype(F32)).astype(BF16)
                h2s[h, di, rest, :] = own[rest]

            task(("s2h", h, d, "go"), deps=[("s2q", h, d), ("s1", h, d)], run=second, sends=[("s2h", h, d)], cost=0.08, prio=2)

        def last(h=h):
            total = s1[h, 0].astype(F32) + h2[h, 0].astype(F32) + h2[h, 1].astype(F32)
            gin_out[h * 2 * quarter : (h + 1) * 2 * quarter, :] = total.astype(BF16)

        task(("gin", h), deps=[("s2h", h, 1), ("s2h", h, -1), ("s1", h, 0)], run=last, cost=0.1, prio=8)

    for q in range(4):
        for i in range(3):
            wst[q, :, i * 128 : (i + 1) * 128] = w3[i, :, q * 128 : (q + 1) * 128]
    for i in range(3):
        wb[z, r, :, i * 128 : (i + 1) * 128] = w3[i, :, lanes(r)]
    k_me, _ = place("x", 0, 0)
    tok[k_me, r] = tokens[...]
    go[r] = gout[:, lanes(r)]
    acc[...] = jnp.zeros_like(acc)
    sfs[...] = jnp.zeros_like(sfs)
    barrier = pltpu.get_barrier_semaphore()
    peers = [at_z(e) for e in offsets] + [at_quad(m) for m in (1, 2, 3)] + [at_xy(a, d) for a in ("x", "y") for d in SIGNS]
    for peer in peers:
        pl.semaphore_signal(barrier, inc=1, device_id=peer, device_id_type=MESH)
    pl.semaphore_wait(barrier, len(peers))

    order, _ = planned_order(tasks, msgs)
    waited = set()
    for step in order:
        for dep in step["deps"]:
            if dep in msgs and dep not in waited:
                copy_of(dep).wait_recv()
                waited.add(dep)
        if step["run"] is not None:
            step["run"]()
        for name in step["sends"]:
            copy_of(name).start()
    for name in msgs:
        copy_of(name).wait_send()


def scratch(nz, rows, cols, n_messages):
    ntok = 4 * rows
    quarter = rows // 4
    v = pltpu.VMEM
    return [
        v((nz, 4, rows, cols), BF16),
        v((4, 128, 384), BF16),
        v((nz, 4, 128, 384), BF16),
        v((4, rows, 128), BF16),
        v((4, rows, 384), F32),
        v((3, 8, 16, ntok + 512), BF16),
        v((8, 16, ntok + 256), BF16),
        v((8, 256, 128), BF16),
        v((8, 128, 256), BF16),
        v((4, 8, 128), F32),
        v((128, 128), F32),
        v((8, 16, ntok), BF16),
        v((ntok, 128), BF16),
        v((4, rows, 128), BF16),
        v((3, 8, 16, ntok), BF16),
        v((ntok, 384), BF16),
        v((8, 128), F32),
        v((128, 128), F32),
        v((24, 128), F32),
        v((nz - 1, 24, 128), F32),
        v((24, 128), F32),
        v((3, 24, 128), F32),
        v((nz, 4, 384, 128), F32),
        v((4 * (nz - 1), 384, 128), BF16),
        v((4 * (nz - 1), 384, 128), BF16),
        v((3, 384, 128), BF16),
        v((3, 384, 128), BF16),
        v((8, 4, rows, cols), BF16),
        v((8, 2, rows, cols), BF16),
        v((2, 4, 2, quarter, cols), BF16),
        v((2, 4, 2, 2 * quarter, cols), BF16),
        v((2, 4, 2, 2 * quarter, cols), BF16),
        v((2, 4, 2 * quarter, cols), BF16),
        v((2, 2, quarter, cols), BF16),
        v((2, 2, 2 * quarter, cols), BF16),
        v((2, 2, 2 * quarter, cols), BF16),
        pltpu.SemaphoreType.DMA((n_messages,)),
        pltpu.SemaphoreType.DMA((n_messages,)),
    ]


def per_device(tokens, in_weight, short_filter, long_filter, grad_out):
    rows, cols = tokens.shape
    nz = lax.axis_size("dp") // 4
    scale = float(rows * 4 * nz) ** (-0.5)
    vmem = pl.BlockSpec(memory_space=pltpu.VMEM)

    def body(*refs):
        block_kernel(*refs, nz=nz, scale=scale)

    mixed, grad_in, grad_w, grad_long, grad_short = pl.pallas_call(
        body,
        out_shape=(
            jax.ShapeDtypeStruct((rows, cols), BF16),
            jax.ShapeDtypeStruct((rows, cols), BF16),
            jax.ShapeDtypeStruct((3, 128, cols), F32),
            jax.ShapeDtypeStruct((32, 128), F32),
            jax.ShapeDtypeStruct((3, 3, cols), F32),
        ),
        in_specs=[vmem] * 5,
        out_specs=(vmem,) * 5,
        scratch_shapes=scratch(nz, rows, cols, 256),
        compiler_params=pltpu.CompilerParams(
            collective_id=0, has_side_effects=True, vmem_limit_bytes=62 * 1024 * 1024
        ),
        name="hyena_block",
    )(tokens, in_weight.transpose(1, 0, 2), short_filter, long_filter, grad_out)
    return mixed, grad_in, grad_w.transpose(1, 0, 2), grad_long, grad_short


def solution(mesh):
    placed = (
        P("dp", ("row", "col")),
        P("dp", None, ("row", "col")),
        P(None, None, ("row", "col")),
        P(("row", "col"), None),
        P("dp", ("row", "col")),
    )
    return jax.shard_map(
        per_device,
        mesh=mesh,
        in_specs=placed,
        out_specs=(
            P("dp", ("row", "col")),
            P("dp", ("row", "col")),
            P("dp", None, ("row", "col")),
            P(("row", "col"), None),
            P(None, None, ("row", "col")),
        ),
        check_vma=False,
    )
```

time: 540 us -> 129 us (0.24)
  waiting for transfers between devices: 204 us -> 0 us
  local copies, waits for them, and re-layouts: 137 us -> 5.54 us
  blocking collectives: 125 us -> 0 us
  Pallas kernels: 0 us -> 123 us
  matrix products: 39.5 us -> 0 us
  between operations: 14 us -> 0.65 us
  other arithmetic: 10.2 us -> 0 us
  starting transfers between devices: 6.82 us -> 0 us
    all_gather x2 -> x0, waiting for transfers between devices: 170 us -> none  [the longest x1 120 us: per_device(): full_w = lax.all_gather(in_weight, 'dp', axis=0, tiled=True)]
    psum x1 -> x0, blocking collectives: 125 us -> none  [per_device(): lax.psum(filter_part.astype(jnp.bfloat16), 'dp').astype(jnp.float32)]
    pallas_call x0 -> x1, Pallas kernels: none -> 123 us  [per_device(): pl.pallas_call(body, out_shape=(jax.ShapeDtypeStruct((rows, cols), BF16),...]
    reshape x6 -> x0, local copies, waits for them, and re-layouts: 60.8 us -> none  [the longest x2 30.6 us: toeplitz(): skewed = tiled[:, :rows * (width - 1)].reshape(groups, rows, width - 1)]
    dot_general x6 -> x0, matrix products: 39.5 us -> none  [the longest x1 9.99 us: per_device(): jnp.einsum('sic,dic->sd', grad_mixed, full_w, preferred_element_type=jnp....]
    another operation x4 -> x0, local copies, waits for them, and re-layouts: 29.5 us -> none  [toeplitz(): tiled = jnp.tile(seed_row, (1, rows))]
    reduce_scatter x1 -> x0, waiting for transfers between devices: 28.9 us -> none  [per_device(): lax.psum_scatter(partial_in.astype(jnp.bfloat16), ('row', 'col'), scatter...]
    slice x6 -> x0, local copies, waits for them, and re-layouts: 23.2 us -> none  [the longest x2 11.7 us: toeplitz(): skewed = tiled[:, :rows * (width - 1)].reshape(groups, rows, width - 1)]
  transfers between devices with their start and end apart: 7 -> 0, of which waited for: 4 -> 0; matrix products, arithmetic and copies ran while one was open for 25% -> 0% of each run, Pallas kernels for 0% -> 0%
where the time goes in v1:
time: 129 us
  Pallas kernels  123 us (95%)
  local copies, waits for them, and re-layouts  5.54 us (4%)
    pallas_call x1, Pallas kernels, per_device(): pl.pallas_call(body, out_shape=(jax.ShapeDtypeStruct((rows, cols), BF16),...  123 us
    unnamed x11, local copies, waits for them, and re-layouts  5.54 us

profile of v1, /device:TPU:1, one launch (start us, length us, event | category | flops | bytes accessed | tf_op | source)
XLA Modules:
  0.0 129.3 jit_solution(5513098999220854370)
XLA Ops:
  0.6 123.1 %hyena_block.1 = (bf16[192,512]{1,0:T(8,128)(2,1)}, bf16[192,512]{1,0:T(8,128)(2,1)}, f32[3,128,512]{2,1,0:T(8,128)}, f32[32,128]{1,0:T(8,128)}, f32[3,3,512]{2,1,0:T(4,128)}) custom-call(bf16[192,512]{1,0:T(8,128)(2,1)} %refs_0_.1, bf16[3,128,512]{2,1,0:T(8,128)(2,1)} %bitcast.3, f32[3,3,512]{2,1,0:T(4,128)} %refs_2_.1, bf16[32,128]{1,0:T(8,128)(2,1)} %refs_3_.1, ...), custom_call_target="tpu_custom_call" | custom-call | tf_op jit(solution)/shard_map/hyena_block/pallas_call | solution.py:594
  123.7 0.0 copy-start
  123.7 1.7 %copy.15 = bf16[192,512]{1,0:T(8,128)(2,1)} copy(bf16[192,512]{1,0:T(8,128)(2,1)} %get-tuple-element.20) | data formatting | bytes 393216
  125.4 1.6 %copy.16 = bf16[192,512]{1,0:T(8,128)(2,1)} copy(bf16[192,512]{1,0:T(8,128)(2,1)} %get-tuple-element.21) | data formatting | bytes 393216
  127.0 0.0 copy-done
  127.1 0.0 copy-start.2
  127.1 0.9 copy.17
  127.9 0.0 copy-done.2
  127.9 0.0 copy-start.1
  127.9 0.6 copy.18
  128.5 0.1 copy-done.1
  128.7 0.6 copy.19
Async XLA Ops:
  123.7 3.3 %copy-start = (f32[3,128,512]{2,1,0:T(8,128)S(1)}, f32[3,128,512]{2,1,0:T(8,128)}, u32[]{:S(2)}) copy-start(f32[3,128,512]{2,1,0:T(8,128)} %get-tuple-element.12) | copy-start | bytes 2359300
  127.1 0.9 copy-start.2
  127.9 0.7 copy-start.1

commit v2 on v1

--- a/solution.py
+++ b/solution.py
@@ -8,6 +8,7 @@
 MESH = pl.DeviceIdType.MESH
 F32, BF16 = jnp.float32, jnp.bfloat16
 SIGNS = (1, -1)
+UNROLL = 1
 LINK_RATE = {"z": 46.0e3, "x": 46.0e3, "y": 46.0e3, "d": 200.0e3}
 LINK_LATENCY = {"z": 1.6, "x": 1.6, "y": 1.6, "d": 1.0}
 
@@ -44,8 +45,8 @@
 
 def block_kernel(
     tokens, w3, sf, lf, gout, mixed_out, gin_out, gw_out, gl_out, gs_out,
-    tok, wst, wb, go, acc, mx, gox, toe, voe, lfs, sfs, mxo, mxt, mr, gmt, gm,
-    glb, gsb, smv, smr, smt, sqr, gp, ws, wr, fs, fr, pp, pr, q1, h1s, h1, s1, q2, h2s, h2,
+    tok, wst, wb, go, acc, before, after, edge, mx, gox, toe, voe, lfs, sfs, mxo, mxt, mr, gmt, gm,
+    gcs, pds, gfs, glb, gsb, smv, smr, smt, sqr, gp, ws, wr, fs, fr, pp, pr, q1, h1s, h1, s1, q2, h2s, h2,
     ssem, rsem, *, nz, scale,
 ):
     dp, y, xl = lax.axis_index("dp"), lax.axis_index("row"), lax.axis_index("col")
@@ -168,17 +169,17 @@
     task("tok_first", deps=[("tok1", 0), ("tok1", 1)], prio=0)
     task("tok_all", deps=token_msgs, prio=4)
 
+    started = []
+
     def first_matmul(e, far):
         zs = wrap(z - e, nz)
         hf = 1 - xh if far else xh
 
-        def tile(rr, carry):
-            lhs = tok[zs, rr, :, pl.ds(pl.multiple_of(hf * 256, 256), 256)]
-            rhs = wb[zs, pl.ds(hf * 2, 2)].reshape(256, 384)
-            acc[rr] += jnp.dot(lhs, rhs, preferred_element_type=F32)
-            return carry
-
-        lax.fori_loop(0, 4, tile, 0)
+        lhs = tok[zs, :, :, pl.ds(pl.multiple_of(hf * 256, 256), 256)].reshape(ntok, 256)
+        rhs = wb[zs, pl.ds(hf * 2, 2)].reshape(256, 384)
+        out = jnp.dot(lhs, rhs, preferred_element_type=F32)
+        acc[...] = out + acc[...] if started else out
+        started.append(e)
 
     mm = []
     for far in (False, True):
@@ -191,7 +192,7 @@
                 deps = [("w", m, d, half_z) for m in pair]
             else:
                 deps = [("w", m, 1 if e > 0 else -1, abs(e)) for m in pair]
-            mm.append(task(("mm", e, far), deps=["tok_all"] + deps, run=lambda e=e, far=far: first_matmul(e, far), cost=0.55, prio=6))
+            mm.append(task(("mm", e, far), deps=["tok_all"] + deps, run=lambda e=e, far=far: first_matmul(e, far), cost=0.45, prio=6))
 
     def build_toeplitz():
         for q in range(4):
@@ -220,46 +221,57 @@
     msg("goh", lambda: gox.at[:, :, pl.ds(0, 256)], lambda: gox.at[:, :, pl.ds(ntok, 256)], lambda: at_z(-1), "z-", 128 * 512)
     task("got", deps=[("goq", 1), ("goq", 2), ("goq", 3)], run=turn_gout, sends=["goh"], cost=0.6, prio=7)
 
+    def edge_rows():
+        edge[0] = acc[0:144, :].astype(BF16)
+        edge[1] = acc[ntok - 144 : ntok, :].astype(BF16)
+
+    key, first = pl.ds(128, 256), pl.ds(0, 128)
+    msg(("mh", 1, 1), lambda: edge.at[1, :, key], lambda: before.at[pl.ds(112, 144), key], lambda: at_z(1), "z+", 144 * 512)
+    msg(("mh", 1, 0), lambda: edge.at[1, pl.ds(128, 16), first], lambda: before.at[pl.ds(240, 16), first], lambda: at_z(1), "z+", 16 * 256)
+    msg(("mh", -1, 0), lambda: edge.at[0, :, first], lambda: after.at[pl.ds(0, 144), first], lambda: at_z(-1), "z-", 144 * 256)
+    msg(("mh", -1, 1), lambda: edge.at[0, pl.ds(0, 16), key], lambda: after.at[pl.ds(0, 16), key], lambda: at_z(-1), "z-", 16 * 512)
+    halos = [("mh", 1, 1), ("mh", 1, 0), ("mh", -1, 0), ("mh", -1, 1)]
+    task("edge", deps=mm, run=edge_rows, sends=halos, cost=0.1, prio=0)
+
     def turn_mixed():
         for i in range(3):
-            flat = acc[:, :, i * 128 : (i + 1) * 128].reshape(ntok, 128).astype(BF16).T
+            flat = acc[:, i * 128 : (i + 1) * 128].astype(BF16).T
             mx[i, :, :, 256 : 256 + ntok] = flat.reshape(ngroups, members, ntok)
 
-    msg(("mh", 1), lambda: mx.at[:, :, :, pl.ds(ntok, 256)], lambda: mx.at[:, :, :, pl.ds(0, 256)], lambda: at_z(1), "z+", 384 * 512)
-    msg(("mh", -1), lambda: mx.at[:, :, :, pl.ds(256, 256)], lambda: mx.at[:, :, :, pl.ds(256 + ntok, 256)], lambda: at_z(-1), "z-", 384 * 512)
-    task("mxt", deps=mm, run=turn_mixed, sends=[("mh", 1), ("mh", -1)], cost=1.5, prio=0)
+    task("mxt", deps=["edge"], run=turn_mixed, cost=0.4, prio=0)
+
+    def turn_halos():
+        for i in range(3):
+            for buf, off, dead in ((before, 0, z == 0), (after, 256 + ntok, z == nz - 1)):
+                flat = buf[:, i * 128 : (i + 1) * 128].T
+                mx[i, :, :, off : off + 256] = jnp.where(dead, jnp.zeros_like(flat), flat).reshape(ngroups, members, 256)
+        ahead = gox[:, :, ntok : ntok + 256]
+        gox[:, :, ntok : ntok + 256] = jnp.where(z == nz - 1, jnp.zeros_like(ahead), ahead)
+
+    task("halo", deps=halos + ["goh", "mxt", "got"], run=turn_halos, cost=0.3, prio=0)
 
     span = ntok + 128
 
+    def tap_of(g):
+        taps = sfs[pl.ds(pl.multiple_of(g * members, members), members), :]
+        return lambda j, i: taps[:, 3 * j + i : 3 * j + i + 1]
+
     def local_operator():
-        lane = lax.broadcasted_iota(jnp.int32, (members, 128), 1)
-        flip = (
-            lax.broadcasted_iota(jnp.int32, (128, 128), 0) + lax.broadcasted_iota(jnp.int32, (128, 128), 1) == 127
-        ).astype(F32).astype(BF16)
-        width = ntok + 512
-        position = lax.broadcasted_iota(jnp.int32, (members, width), 1)
-        low = jnp.where(z == 0, 256, 0)
-        high = jnp.where(z == nz - 1, 256 + ntok, width)
-        inside = (position >= low) & (position < high)
-
         def group(g, carry):
-            taps = sfs[pl.ds(pl.multiple_of(g * members, members), members), :]
-
-            def tap(j, i):
-                return taps[:, 3 * j + i : 3 * j + i + 1]
-
-            lag, feats = [], []
+            tap = tap_of(g)
+            feats = []
             for i in range(3):
-                base = jnp.where(inside, mx[i, g].astype(F32), 0.0)
-                lag.append([base, pltpu.roll(base, 1, 1), pltpu.roll(base, 2, 1)])
-                feats.append(tap(0, i) * lag[i][0] + tap(1, i) * lag[i][1] + tap(2, i) * lag[i][2])
+                base = mx[i, g].astype(F32)
+                feats.append(tap(0, i) * base + tap(1, i) * pltpu.roll(base, 1, 1) + tap(2, i) * pltpu.roll(base, 2, 1))
             product = (feats[1] * feats[2]).astype(BF16)
+            pds[g] = product
             windows = jnp.concatenate([product[:, 128 * (b + 1) : 128 * (b + 3)] for b in range(nblocks + 1)], axis=0)
             out = jnp.dot(windows, toe[g], preferred_element_type=F32)
             conv = jnp.concatenate([out[members * b : members * (b + 1)] for b in range(nblocks + 1)], axis=1)
-            up = jnp.where(inside[:, 256:], gox[g].astype(F32), 0.0)
+            up = gox[g].astype(F32)
             query = feats[0][:, 256:]
             gconv = (up * query).astype(BF16)
+            gcs[g] = gconv[:, :ntok]
             ahead = jnp.concatenate([gconv[:, 128 * b : 128 * (b + 2)] for b in range(nblocks + 1)], axis=0)
             back = lax.dot_general(ahead, voe[g], (((1,), (1,)), ((), ())), preferred_element_type=F32)
             gproduct = jnp.concatenate([back[members * b : members * (b + 1)] for b in range(nblocks + 1)], axis=1)
@@ -269,30 +281,45 @@
                 gproduct * feats[2][:, 256 : 256 + span],
                 gproduct * feats[1][:, 256 : 256 + span],
             ]
-            sums = jnp.zeros((members, 128), F32)
             for i in range(3):
                 grad = tap(0, i) * gfeats[i] + tap(1, i) * pltpu.roll(gfeats[i], span - 1, 1) + tap(2, i) * pltpu.roll(gfeats[i], span - 2, 1)
                 gmt[i, g] = grad[:, :ntok].astype(BF16)
+                gfs[i, g] = gfeats[i][:, :ntok]
+            return carry
+
+        lax.fori_loop(0, ngroups, group, 0, unroll=UNROLL)
+
+    task("local", deps=["halo", "toe"], run=local_operator, cost=6.0, prio=0)
+
+    def filter_sums():
+        lane = lax.broadcasted_iota(jnp.int32, (members, 128), 1)
+        flip = (
+            lax.broadcasted_iota(jnp.int32, (128, 128), 0) + lax.broadcasted_iota(jnp.int32, (128, 128), 1) == 127
+        ).astype(F32).astype(BF16)
+
+        def group(g, carry):
+            sums = jnp.zeros((members, 128), F32)
+            for i in range(3):
+                base = mx[i, g, :, 128 : 256 + ntok].astype(F32)
                 for j in range(3):
-                    both = gfeats[i][:, :ntok] * lag[i][j][:, 256 : 256 + ntok]
+                    late = pltpu.roll(base, j, 1) if j else base
+                    both = gfs[i, g] * late[:, 128:]
                     part = both[:, 0:128]
                     for b in range(1, nblocks):
                         part = part + both[:, 128 * b : 128 * (b + 1)]
                     sums = jnp.where(lane == 3 * j + i, jnp.sum(part, axis=1, keepdims=True), sums)
             gsb[pl.ds(pl.multiple_of(g * members, members), members), :] = sums
-            held = jnp.concatenate([gconv[:, 128 * b : 128 * (b + 1)] for b in range(nblocks)], axis=0)
+            windows = jnp.concatenate([pds[g, :, 128 * (b + 1) : 128 * (b + 3)] for b in range(nblocks)], axis=0)
+            held = jnp.concatenate([gcs[g, :, 128 * b : 128 * (b + 1)] for b in range(nblocks)], axis=0)
             flipped = jnp.dot(held, flip, preferred_element_type=F32).astype(BF16)
-            pairs = lax.dot_general(flipped, windows[: members * nblocks], (((0,), (0,)), ((), ())), preferred_element_type=F32)
+            pairs = lax.dot_general(flipped, windows, (((0,), (0,)), ((), ())), preferred_element_type=F32)
             skew = pltpu.roll(pairs, 0, 1, stride=1, stride_axis=0)
             glb[pl.ds(g, 1), :] = jnp.sum(skew, axis=0, keepdims=True)[:, 128:]
             return carry
 
         lax.fori_loop(0, ngroups, group, 0)
-        unflipped = jnp.dot(glb[...].astype(BF16), flip, preferred_element_type=F32)
-        smv[0:8, :] = unflipped
+        smv[0:8, :] = jnp.dot(glb[...].astype(BF16), flip, preferred_element_type=F32)
         smv[8:24, :] = gsb[...].T[0:16, :]
-
-    task("local", deps=[("mh", 1), ("mh", -1), "goh", "toe", "got", "mxt"], run=local_operator, cost=9.0, prio=0)
 
     for m in (1, 2, 3):
         link, hops = ("d", 1) if m == 1 else ("x-", 2)
@@ -306,11 +333,11 @@
         for g in range(ngroups):
             mxt[:, g * members : (g + 1) * members] = mxo[g].T
 
-    task("mixed_send", deps=["local"], run=turn_output, sends=[("mq", m) for m in (1, 2, 3)], cost=0.7, prio=3.35)
+    task("mixed_send", deps=["local"], run=turn_output, sends=[("mq", m) for m in (1, 2, 3)], cost=0.3, prio=3.35)
     offsets = [e for e in range(-half_z + 1, half_z + 1) if e]
     for n, e in enumerate(offsets):
         msg(("sm", e), lambda: smv, lambda n=n: smr.at[n], lambda e=e: at_z(e), "z+" if e > 0 else "z-", 24 * 512, abs(e))
-    task("small_send", deps=["local"], sends=[("sm", e) for e in offsets], prio=3.36)
+    task("small_send", deps=["local"], run=filter_sums, cost=4.0, sends=[("sm", e) for e in offsets], prio=3.9)
 
     def small_total():
         total = smv[...]
@@ -339,23 +366,16 @@
 
     def weight_partial(e):
         zc = wrap(z + e, nz)
-        lhs = gmt[...].reshape(384, ntok)
-
-        def tile(n, carry):
-            rhs = tok[zc, :, :, pl.ds(pl.multiple_of(n * 256, 256), 256)].reshape(ntok, 256)
-            out = jnp.dot(lhs, rhs, preferred_element_type=F32)
-            gp[e % nz, 2 * n] = out[:, 0:128]
-            gp[e % nz, 2 * n + 1] = out[:, 128:256]
-            return carry
-
-        lax.fori_loop(0, 2, tile, 0)
+        out = jnp.dot(gmt[...].reshape(384, ntok), tok[zc].reshape(ntok, cols), preferred_element_type=F32)
+        for n in range(4):
+            gp[e % nz, n] = out[:, n * 128 : (n + 1) * 128]
 
     chunks = [half_z]
     for e in range(half_z - 1, 0, -1):
         chunks += [e, -e]
     chunks.append(0)
     for n, e in enumerate(chunks):
-        task(("gw", e % nz), deps=["local"], run=lambda e=e: weight_partial(e), cost=1.0, prio=3 + 0.1 * n)
+        task(("gw", e % nz), deps=["local"], run=lambda e=e: weight_partial(e), cost=0.6, prio=3 + 0.1 * n)
     slot = {}
     for m in range(4):
         for d in SIGNS:
@@ -406,14 +426,8 @@
 
     def token_partial(dy, dx):
         k = feature_block(dy, dx)
-        rhs = wb[k].reshape(512, 384)
-
-        def tile(rr, carry):
-            lhs = gm[pl.ds(pl.multiple_of(rr * rows, rows), rows), :]
-            pp[k, rr] = lax.dot_general(lhs, rhs, (((1,), (1,)), ((), ())), preferred_element_type=F32).astype(BF16)
-            return carry
-
-        lax.fori_loop(0, 4, tile, 0)
+        out = lax.dot_general(gm[...], wb[k].reshape(512, 384), (((1,), (1,)), ((), ())), preferred_element_type=F32)
+        pp[k] = out.astype(BF16).reshape(4, rows, cols)
 
     def pair_sum(dy, dx):
         k = feature_block(dy, dx)
@@ -424,7 +438,7 @@
         for i in range(3):
             gm[:, i * 128 : (i + 1) * 128] = gmt[i].reshape(128, ntok).T
 
-    task("turn_grad", deps=["local"], run=turn_grad, cost=1.0, prio=3.15)
+    task("turn_grad", deps=["local"], run=turn_grad, cost=0.3, prio=3.15)
     for n, dy in enumerate((2, 1, -1, 0)):
         for dx in (0, 1):
             both = [
@@ -434,7 +448,7 @@
                 )
                 for ph in range(2)
             ]
-            task(("pk", dy, dx), deps=["turn_grad"], run=lambda dy=dy, dx=dx: token_partial(dy, dx), sends=both, cost=1.1, prio=3.21 + 0.12 * n + 0.06 * dx)
+            task(("pk", dy, dx), deps=["turn_grad"], run=lambda dy=dy, dx=dx: token_partial(dy, dx), sends=both, cost=0.75, prio=3.21 + 0.12 * n + 0.06 * dx)
             task(("pa", dy, dx), deps=both + [("pk", dy, dx)], run=lambda dy=dy, dx=dx: pair_sum(dy, dx), cost=0.25, prio=2.5)
 
     def part_rows(h, part):
@@ -513,10 +527,11 @@
     k_me, _ = place("x", 0, 0)
     tok[k_me, r] = tokens[...]
     go[r] = gout[:, lanes(r)]
-    acc[...] = jnp.zeros_like(acc)
+    before[...] = jnp.zeros_like(before)
+    after[...] = jnp.zeros_like(after)
     sfs[...] = jnp.zeros_like(sfs)
     barrier = pltpu.get_barrier_semaphore()
-    peers = [at_z(e) for e in offsets] + [at_quad(m) for m in (1, 2, 3)] + [at_xy(a, d) for a in ("x", "y") for d in SIGNS]
+    peers = [at_z(e) for e in SIGNS] + [at_quad(m) for m in (1, 2, 3)] + [at_xy(a, d) for a in ("x", "y") for d in SIGNS]
     for peer in peers:
         pl.semaphore_signal(barrier, inc=1, device_id=peer, device_id_type=MESH)
     pl.semaphore_wait(barrier, len(peers))
@@ -545,7 +560,10 @@
         v((4, 128, 384), BF16),
         v((nz, 4, 128, 384), BF16),
         v((4, rows, 128), BF16),
-        v((4, rows, 384), F32),
+        v((ntok, 384), F32),
+        v((256, 384), BF16),
+        v((256, 384), BF16),
+        v((2, 144, 384), BF16),
         v((3, 8, 16, ntok + 512), BF16),
         v((8, 16, ntok + 256), BF16),
         v((8, 256, 128), BF16),
@@ -557,6 +575,9 @@
         v((4, rows, 128), BF16),
         v((3, 8, 16, ntok), BF16),
         v((ntok, 384), BF16),
+        v((8, 16, ntok), BF16),
+        v((8, 16, ntok + 512), BF16),
+        v((3, 8, 16, ntok), F32),
         v((8, 128), F32),
         v((128, 128), F32),
         v((24, 128), F32),
@@ -591,7 +612,7 @@
     def body(*refs):
         block_kernel(*refs, nz=nz, scale=scale)
 
-    mixed, grad_in, grad_w, grad_long, grad_short = pl.pallas_call(
+    results = pl.pallas_call(
         body,
         out_shape=(
             jax.ShapeDtypeStruct((rows, cols), BF16),
@@ -608,6 +629,18 @@
         ),
         name="hyena_block",
     )(tokens, in_weight.transpose(1, 0, 2), short_filter, long_filter, grad_out)
+
+    def hand_over(*refs):
+        for source, target in zip(refs[:5], refs[5:]):
+            target[...] = source[...]
+
+    mixed, grad_in, grad_w, grad_long, grad_short = pl.pallas_call(
+        hand_over,
+        out_shape=tuple(jax.ShapeDtypeStruct(a.shape, a.dtype) for a in results),
+        in_specs=[vmem] * 5,
+        out_specs=(vmem,) * 5,
+        name="hand_over",
+    )(*results)
     return mixed, grad_in, grad_w.transpose(1, 0, 2), grad_long, grad_short
 
 

time: 129 us -> 113 us (0.88)
  Pallas kernels: 123 us -> 112 us
  local copies, waits for them, and re-layouts: 5.54 us -> 0 us
    pallas_call x1, Pallas kernels: 123 us -> 109 us  [per_device(): pl.pallas_call(body, out_shape=(jax.ShapeDtypeStruct((rows, cols), BF16),...]
    unnamed x11 -> x0, local copies, waits for them, and re-layouts: 5.54 us -> none
    pallas_call x0 -> x1, Pallas kernels: none -> 2.39 us  [per_device(): pl.pallas_call(hand_over, out_shape=tuple((jax.ShapeDtypeStruct(a.shape,...]
where the time goes in v2:
time: 113 us; the launch traced here: 112 us
  Pallas kernels  112 us (99%)
    pallas_call x1, Pallas kernels, per_device(): pl.pallas_call(body, out_shape=(jax.ShapeDtypeStruct((rows, cols), BF16),...  109 us
    pallas_call x1, Pallas kernels, per_device(): pl.pallas_call(hand_over, out_shape=tuple((jax.ShapeDtypeStruct(a.shape,...  2.39 us

profile of v2, /device:TPU:1, one launch (start us, length us, event | category | flops | bytes accessed | tf_op | source)
XLA Modules:
  0.0 112.2 jit_solution(12020819919479164874)
XLA Ops:
  0.6 109.2 %hyena_block.1 = (bf16[192,512]{1,0:T(8,128)(2,1)}, bf16[192,512]{1,0:T(8,128)(2,1)}, f32[3,128,512]{2,1,0:T(8,128)}, f32[32,128]{1,0:T(8,128)}, f32[3,3,512]{2,1,0:T(4,128)}) custom-call(bf16[192,512]{1,0:T(8,128)(2,1)} %refs_0_.1, bf16[3,128,512]{2,1,0:T(8,128)(2,1)} %bitcast.2, f32[3,3,512]{2,1,0:T(4,128)} %refs_2_.1, bf16[32,128]{1,0:T(8,128)(2,1)} %refs_3_.1, ...), custom_call_target="tpu_custom_call" | custom-call | tf_op jit(solution)/shard_map/hyena_block/pallas_call | solution.py:615
  109.8 2.4 %hand_over.1 = (bf16[192,512]{1,0:T(8,128)(2,1)}, bf16[192,512]{1,0:T(8,128)(2,1)}, f32[3,128,512]{2,1,0:T(8,128)}, f32[32,128]{1,0:T(8,128)}, f32[3,3,512]{2,1,0:T(4,128)}) custom-call(bf16[192,512]{1,0:T(8,128)(2,1)} %get-tuple-element.15.refs_0_, bf16[192,512]{1,0:T(8,128)(2,1)} %get-tuple-element.16.refs_1_, f32[3,128,512]{2,1,0:T(8,128)} %get-tuple-element.17.refs_2_, ...), custom_call_target="tpu_custom_call" | custom-call | tf_op jit(solution)/shard_map/hand_over/pallas_call | solution.py:637

commit v3 on v2

--- a/solution.py
+++ b/solution.py
@@ -9,7 +9,7 @@
 F32, BF16 = jnp.float32, jnp.bfloat16
 SIGNS = (1, -1)
 UNROLL = 1
-LINK_RATE = {"z": 46.0e3, "x": 46.0e3, "y": 46.0e3, "d": 200.0e3}
+LINK_RATE = {"z": 46.0e3, "x": 46.0e3, "y": 46.0e3, "d": 600.0e3}
 LINK_LATENCY = {"z": 1.6, "x": 1.6, "y": 1.6, "d": 1.0}
 
 
@@ -37,23 +37,26 @@
         order.append(task)
         for name in task["sends"]:
             link, nbytes, hops = msgs[name]["link"], msgs[name]["bytes"], msgs[name]["hops"]
-            begin = max(now, link_free.get(link, 0.0))
-            link_free[link] = begin + nbytes * hops / LINK_RATE[link[0]]
-            arrival[name] = link_free[link] + LINK_LATENCY[link[0]] * hops
+            arrival[name] = 0.0
+            for one in ("x+", "x-") if link == "x2" else (link,):
+                load = nbytes * (1 if link == "x2" else hops)
+                begin = max(now, link_free.get(one, 0.0))
+                link_free[one] = begin + load / LINK_RATE[one[0]]
+                arrival[name] = max(arrival[name], link_free[one] + LINK_LATENCY[one[0]] * hops)
     return order, now
 
 
 def block_kernel(
-    tokens, w3, sf, lf, gout, mixed_out, gin_out, gw_out, gl_out, gs_out,
-    tok, wst, wb, go, acc, before, after, edge, mx, gox, toe, voe, lfs, sfs, mxo, mxt, mr, gmt, gm,
-    gcs, pds, gfs, glb, gsb, smv, smr, smt, sqr, gp, ws, wr, fs, fr, pp, pr, q1, h1s, h1, s1, q2, h2s, h2,
-    ssem, rsem, *, nz, scale,
+    tokens_hbm, w3_hbm, sf_hbm, lf_hbm, gout_hbm, mixed_out, gin_out, gw_out, gl_out, gs_out,
+    w3, sf, lf, gout, tok, wst, wb, go, acc, before, after, edge, mx, gox, toe, voe, lfs, sfs, mxo, mxt, mr, gmt, gm,
+    gcs, pds, gfs, glb, gsb, own_sums, smv, smr, smt, sqr, gp, ws, wr, fs, fr, pp, pr, q1, h1s, h1, s1, q2, h2s, h2,
+    ssem, rsem, insem, *, nz, scale,
 ):
     dp, y, xl = lax.axis_index("dp"), lax.axis_index("row"), lax.axis_index("col")
     z, r = dp // 4, dp % 4
     xh, c = r // 2, r % 2
     x = xh * 2 + xl
-    rows, cols = tokens.shape
+    rows, cols = gout.shape
     quarter = rows // 4
     ntok = 4 * rows
     ngroups, members = mx.shape[1], mx.shape[2]
@@ -108,18 +111,18 @@
 
     wbytes = 128 * 384 * 2
     for m in (1, 2, 3):
-        link, hops = ("d", 1) if m == 1 else ("x+", 2)
+        link, hops = ("d", 1) if m == 1 else ("x2", 2)
         msg(("wq", m), lambda m=m: wst.at[mate(m)], lambda: wb.at[z, r], lambda m=m: at_quad(m), link, wbytes, hops)
         msg(("goq", m), lambda m=m: gout.at[:, lanes(mate(m))], lambda: go.at[r], lambda m=m: at_quad(m), link, rows * 256, hops)
     task("quad_w", sends=[("wq", 1), ("wq", 2), ("wq", 3)], prio=0)
-    task("quad_go", deps=["quad_w", "tok_first"], sends=[("goq", 1), ("goq", 2), ("goq", 3)], prio=1)
-
-    def reach(m, d, gather):
+    task("quad_go", deps=["quad_w", ("t2", 1, 0, 1)], sends=[("goq", 1), ("goq", 2), ("goq", 3)], prio=4)
+
+    def reach(m, d):
         return half_z if (m < 2) == (d > 0) else half_z - 1
 
     for m in range(4):
         for d in SIGNS:
-            for h in range(1, reach(m, d, True) + 1):
+            for h in range(1, reach(m, d) + 1):
                 where = lambda m=m, d=d, h=h: wb.at[wrap(z - d * (h - 1), nz), mate(m)]
                 name = msg(("w", m, d, h), where, where, lambda d=d: at_z(d), "z+" if d > 0 else "z-", wbytes)
                 if h > 1:
@@ -219,7 +222,7 @@
         gox[:, :, 0:ntok] = flat.reshape(ngroups, members, ntok)
 
     msg("goh", lambda: gox.at[:, :, pl.ds(0, 256)], lambda: gox.at[:, :, pl.ds(ntok, 256)], lambda: at_z(-1), "z-", 128 * 512)
-    task("got", deps=[("goq", 1), ("goq", 2), ("goq", 3)], run=turn_gout, sends=["goh"], cost=0.6, prio=7)
+    task("got", deps=[("goq", 1), ("goq", 2), ("goq", 3)], run=turn_gout, sends=["goh"], cost=0.3, prio=3)
 
     def edge_rows():
         edge[0] = acc[0:144, :].astype(BF16)
@@ -289,25 +292,28 @@
 
         lax.fori_loop(0, ngroups, group, 0, unroll=UNROLL)
 
-    task("local", deps=["halo", "toe"], run=local_operator, cost=6.0, prio=0)
-
-    def filter_sums():
+    task("local", deps=["halo", "toe"], run=local_operator, cost=4.5, prio=0)
+
+    def flip_matrix():
+        turned = lax.broadcasted_iota(jnp.int32, (128, 128), 0) + lax.broadcasted_iota(jnp.int32, (128, 128), 1) == 127
+        return turned.astype(F32).astype(BF16)
+
+    def filter_sums(part, size):
         lane = lax.broadcasted_iota(jnp.int32, (members, 128), 1)
-        flip = (
-            lax.broadcasted_iota(jnp.int32, (128, 128), 0) + lax.broadcasted_iota(jnp.int32, (128, 128), 1) == 127
-        ).astype(F32).astype(BF16)
-
-        def group(g, carry):
+        flip = flip_matrix()
+
+        def group(n, carry):
+            g = part * size + n
             sums = jnp.zeros((members, 128), F32)
             for i in range(3):
                 base = mx[i, g, :, 128 : 256 + ntok].astype(F32)
                 for j in range(3):
                     late = pltpu.roll(base, j, 1) if j else base
                     both = gfs[i, g] * late[:, 128:]
-                    part = both[:, 0:128]
+                    total = both[:, 0:128]
                     for b in range(1, nblocks):
-                        part = part + both[:, 128 * b : 128 * (b + 1)]
-                    sums = jnp.where(lane == 3 * j + i, jnp.sum(part, axis=1, keepdims=True), sums)
+                        total = total + both[:, 128 * b : 128 * (b + 1)]
+                    sums = jnp.where(lane == 3 * j + i, jnp.sum(total, axis=1, keepdims=True), sums)
             gsb[pl.ds(pl.multiple_of(g * members, members), members), :] = sums
             windows = jnp.concatenate([pds[g, :, 128 * (b + 1) : 128 * (b + 3)] for b in range(nblocks)], axis=0)
             held = jnp.concatenate([gcs[g, :, 128 * b : 128 * (b + 1)] for b in range(nblocks)], axis=0)
@@ -317,12 +323,19 @@
             glb[pl.ds(g, 1), :] = jnp.sum(skew, axis=0, keepdims=True)[:, 128:]
             return carry
 
-        lax.fori_loop(0, ngroups, group, 0)
-        smv[0:8, :] = jnp.dot(glb[...].astype(BF16), flip, preferred_element_type=F32)
-        smv[8:24, :] = gsb[...].T[0:16, :]
+        lax.fori_loop(0, size, group, 0)
+
+    def filter_pack():
+        own_sums[0:8, :] = jnp.dot(glb[...].astype(BF16), flip_matrix(), preferred_element_type=F32)
+        own_sums[8:24, :] = gsb[...].T[0:16, :]
+        smv[...] = jnp.concatenate([own_sums[...], jnp.zeros((8, 128), F32)], axis=0).astype(BF16)
+
+    parts = 4
+    for n in range(parts):
+        task(("sums", n), deps=["local"], run=lambda n=n: filter_sums(n, ngroups // parts), cost=0.8, prio=(3.21, 3.22, 3.28, 3.29)[n])
 
     for m in (1, 2, 3):
-        link, hops = ("d", 1) if m == 1 else ("x-", 2)
+        link, hops = ("d", 1) if m == 1 else ("x2", 2)
         msg(
             ("mq", m), lambda m=m: mxt.at[pl.ds(pl.multiple_of(mate(m) * rows, rows), rows), :], lambda: mr.at[r],
             lambda m=m: at_quad(m), link, rows * 256, hops,
@@ -333,19 +346,19 @@
         for g in range(ngroups):
             mxt[:, g * members : (g + 1) * members] = mxo[g].T
 
-    task("mixed_send", deps=["local"], run=turn_output, sends=[("mq", m) for m in (1, 2, 3)], cost=0.3, prio=3.35)
+    task("mixed_send", deps=["local"], run=turn_output, sends=[("mq", m) for m in (1, 2, 3)], cost=0.3, prio=3.34)
     offsets = [e for e in range(-half_z + 1, half_z + 1) if e]
     for n, e in enumerate(offsets):
-        msg(("sm", e), lambda: smv, lambda n=n: smr.at[n], lambda e=e: at_z(e), "z+" if e > 0 else "z-", 24 * 512, abs(e))
-    task("small_send", deps=["local"], run=filter_sums, cost=4.0, sends=[("sm", e) for e in offsets], prio=3.9)
+        msg(("sm", e), lambda: smv, lambda n=n: smr.at[n], lambda e=e: at_z(e), "z+" if e > 0 else "z-", 32 * 256, abs(e))
+    task("small_send", deps=[("sums", n) for n in range(parts)], run=filter_pack, sends=[("sm", e) for e in offsets], cost=0.1, prio=3.295)
 
     def small_total():
-        total = smv[...]
+        total = own_sums[...]
         for n in range(len(offsets)):
-            total = total + smr[n]
+            total = total + smr[n, 0:24].astype(F32)
         smt[...] = total * scale
 
-    task("small_sum", deps=[("sm", e) for e in offsets] + ["small_send"], run=small_total, sends=[("sq", m) for m in (1, 2, 3)], cost=0.1, prio=7)
+    task("small", deps=[("sm", e) for e in offsets] + ["small_send"], run=small_total, sends=[("sq", m) for m in (1, 2, 3)], cost=0.1, prio=1)
 
     def small_out():
         for m in range(4):
@@ -355,7 +368,7 @@
             for j in range(3):
                 gs_out[j, :, lanes(q)] = part[8 + 3 * j : 11 + 3 * j]
 
-    task("small_out", deps=[("sq", m) for m in (1, 2, 3)] + ["small_sum"], run=small_out, cost=0.1, prio=9)
+    task("small_out", deps=[("sq", m) for m in (1, 2, 3)] + ["small"], run=small_out, cost=0.1, prio=9)
 
     def mixed_final():
         mixed_out[:, lanes(r)] = mxt[pl.ds(pl.multiple_of(r * rows, rows), rows), :]
@@ -375,22 +388,24 @@
         chunks += [e, -e]
     chunks.append(0)
     for n, e in enumerate(chunks):
-        task(("gw", e % nz), deps=["local"], run=lambda e=e: weight_partial(e), cost=0.6, prio=3 + 0.1 * n)
+        task(("gw", e % nz), deps=["local"], run=lambda e=e: weight_partial(e), cost=0.6, prio=3 + 0.05 * n)
     slot = {}
     for m in range(4):
         for d in SIGNS:
-            top = reach(m, d, False) if m < 2 else reach(m, d, False)
+            top = reach(m, d)
             for h in range(top, 0, -1):
                 slot[m, d, h] = len(slot)
-    for m in (2, 3, 0, 1):
+    for m in (2, 3, 1, 0):
         for d in SIGNS:
-            top = reach(m, d, False)
+            top = reach(m, d)
             for h in range(top, 0, -1):
                 s = slot[m, d, h]
                 name = msg(("wr", m, d, h), lambda s=s: ws.at[s], lambda s=s: wr.at[s], lambda d=d: at_z(d), "z+" if d > 0 else "z-", wbytes)
                 deps = [("gw", (d * h) % nz)]
                 if h < top:
                     deps.append(("wr", m, d, h + 1))
+                elif m < 2:
+                    deps += [("send", "wr", 2, d, 1), ("send", "wr", 3, d, 1)]
 
                 def add(m=m, d=d, h=h, s=s, top=top):
                     value = gp[(d * h) % nz, mate(m)]
@@ -412,7 +427,7 @@
         if m == 0:
             task("wtot0", deps=deps, run=lambda: weight_store(0, weight_total(0)), cost=0.5, prio=8)
             continue
-        link, hops = ("d", 1) if m == 1 else ("x-" if m == 2 else "x+", 2)
+        link, hops = ("d", 1) if m == 1 else ("x2", 2)
         msg(("wf", m), lambda m=m: fs.at[m - 1], lambda m=m: fr.at[m - 1], lambda m=m: at_quad(m), link, wbytes, hops)
 
         def finish(m=m):
@@ -438,7 +453,7 @@
         for i in range(3):
             gm[:, i * 128 : (i + 1) * 128] = gmt[i].reshape(128, ntok).T
 
-    task("turn_grad", deps=["local"], run=turn_grad, cost=0.3, prio=3.15)
+    task("turn_grad", deps=["local"], run=turn_grad, cost=0.3, prio=3.155)
     for n, dy in enumerate((2, 1, -1, 0)):
         for dx in (0, 1):
             both = [
@@ -448,7 +463,7 @@
                 )
                 for ph in range(2)
             ]
-            task(("pk", dy, dx), deps=["turn_grad"], run=lambda dy=dy, dx=dx: token_partial(dy, dx), sends=both, cost=0.75, prio=3.21 + 0.12 * n + 0.06 * dx)
+            task(("pk", dy, dx), deps=["turn_grad"], run=lambda dy=dy, dx=dx: token_partial(dy, dx), sends=both, cost=0.75, prio=(3.16, 3.27, 3.31, 3.36)[n] + 0.01 * dx)
             task(("pa", dy, dx), deps=both + [("pk", dy, dx)], run=lambda dy=dy, dx=dx: pair_sum(dy, dx), cost=0.25, prio=2.5)
 
     def part_rows(h, part):
@@ -519,21 +534,27 @@
 
         task(("gin", h), deps=[("s2h", h, 1), ("s2h", h, -1), ("s1", h, 0)], run=last, cost=0.1, prio=8)
 
+    barrier = pltpu.get_barrier_semaphore()
+    peers = [at_z(e) for e in SIGNS] + [at_quad(m) for m in (1, 2, 3)] + [at_xy(a, d) for a in ("x", "y") for d in SIGNS]
+    for peer in peers:
+        pl.semaphore_signal(barrier, inc=1, device_id=peer, device_id_type=MESH)
+    k_me, _ = place("x", 0, 0)
+    pairs = ((w3_hbm, w3), (tokens_hbm, tok.at[k_me, r]), (gout_hbm, gout), (sf_hbm, sf), (lf_hbm, lf))
+    loads = [pltpu.make_async_copy(source, target, insem.at[n]) for n, (source, target) in enumerate(pairs)]
+    for load in loads:
+        load.start()
+    before[...] = jnp.zeros_like(before)
+    after[...] = jnp.zeros_like(after)
+    loads[0].wait()
     for q in range(4):
         for i in range(3):
             wst[q, :, i * 128 : (i + 1) * 128] = w3[i, :, q * 128 : (q + 1) * 128]
     for i in range(3):
         wb[z, r, :, i * 128 : (i + 1) * 128] = w3[i, :, lanes(r)]
-    k_me, _ = place("x", 0, 0)
-    tok[k_me, r] = tokens[...]
+    for load in loads[1:]:
+        load.wait()
     go[r] = gout[:, lanes(r)]
-    before[...] = jnp.zeros_like(before)
-    after[...] = jnp.zeros_like(after)
     sfs[...] = jnp.zeros_like(sfs)
-    barrier = pltpu.get_barrier_semaphore()
-    peers = [at_z(e) for e in SIGNS] + [at_quad(m) for m in (1, 2, 3)] + [at_xy(a, d) for a in ("x", "y") for d in SIGNS]
-    for peer in peers:
-        pl.semaphore_signal(barrier, inc=1, device_id=peer, device_id_type=MESH)
     pl.semaphore_wait(barrier, len(peers))
 
     order, _ = planned_order(tasks, msgs)
@@ -556,6 +577,10 @@
     quarter = rows // 4
     v = pltpu.VMEM
     return [
+        v((3, 128, cols), BF16),
+        v((3, 3, cols), F32),
+        v((32, 128), BF16),
+        v((rows, cols), BF16),
         v((nz, 4, rows, cols), BF16),
         v((4, 128, 384), BF16),
         v((nz, 4, 128, 384), BF16),
@@ -581,7 +606,8 @@
         v((8, 128), F32),
         v((128, 128), F32),
         v((24, 128), F32),
-        v((nz - 1, 24, 128), F32),
+        v((32, 128), BF16),
+        v((nz - 1, 32, 128), BF16),
         v((24, 128), F32),
         v((3, 24, 128), F32),
         v((nz, 4, 384, 128), F32),
@@ -600,6 +626,7 @@
         v((2, 2, 2 * quarter, cols), BF16),
         pltpu.SemaphoreType.DMA((n_messages,)),
         pltpu.SemaphoreType.DMA((n_messages,)),
+        pltpu.SemaphoreType.DMA((5,)),
     ]
 
 
@@ -615,13 +642,13 @@
     results = pl.pallas_call(
         body,
         out_shape=(
-            jax.ShapeDtypeStruct((rows, cols), BF16),
-            jax.ShapeDtypeStruct((rows, cols), BF16),
-            jax.ShapeDtypeStruct((3, 128, cols), F32),
-            jax.ShapeDtypeStruct((32, 128), F32),
-            jax.ShapeDtypeStruct((3, 3, cols), F32),
+            pltpu.VMEM((rows, cols), BF16),
+            pltpu.VMEM((rows, cols), BF16),
+            pltpu.VMEM((3, 128, cols), F32),
+            pltpu.VMEM((32, 128), F32),
+            pltpu.VMEM((3, 3, cols), F32),
         ),
-        in_specs=[vmem] * 5,
+        in_specs=[pl.BlockSpec(memory_space=pl.ANY)] * 5,
         out_specs=(vmem,) * 5,
         scratch_shapes=scratch(nz, rows, cols, 256),
         compiler_params=pltpu.CompilerParams(
@@ -631,16 +658,21 @@
     )(tokens, in_weight.transpose(1, 0, 2), short_filter, long_filter, grad_out)
 
     def hand_over(*refs):
-        for source, target in zip(refs[:5], refs[5:]):
-            target[...] = source[...]
+        sems = refs[-1]
+        copies = [pltpu.make_async_copy(a, b, sems.at[n]) for n, (a, b) in enumerate(zip(refs[:5], refs[5:10]))]
+        for copy in copies:
+            copy.start()
+        for copy in copies:
+            copy.wait()
 
     mixed, grad_in, grad_w, grad_long, grad_short = pl.pallas_call(
         hand_over,
         out_shape=tuple(jax.ShapeDtypeStruct(a.shape, a.dtype) for a in results),
         in_specs=[vmem] * 5,
-        out_specs=(vmem,) * 5,
+        out_specs=(pl.BlockSpec(memory_space=pl.ANY),) * 5,
+        scratch_shapes=[pltpu.SemaphoreType.DMA((5,))],
         name="hand_over",
-    )(*results)
+    )(*[pltpu.with_memory_space_constraint(a, pltpu.VMEM) for a in results])
     return mixed, grad_in, grad_w.transpose(1, 0, 2), grad_long, grad_short
 
 

time: 113 us -> 98.5 us (0.87)
  Pallas kernels: 112 us -> 95.9 us
    pallas_call x1, Pallas kernels: 109 us -> 94.8 us  [per_device(): pl.pallas_call(body, out_shape=(pltpu.VMEM((rows, cols), BF16), pltpu.VME...]
    pallas_call x1, Pallas kernels: 2.39 us -> 1.06 us  [per_device(): pl.pallas_call(hand_over, out_shape=tuple((jax.ShapeDtypeStruct(a.shape,...]
where the time goes in v3:
time: 98.5 us; the launch traced here: 96.7 us
  Pallas kernels  95.9 us (97%)
    pallas_call x1, Pallas kernels, per_device(): pl.pallas_call(body, out_shape=(pltpu.VMEM((rows, cols), BF16), pltpu.VME...  94.8 us

profile of v3, /device:TPU:1, one launch (start us, length us, event | category | flops | bytes accessed | tf_op | source)
XLA Modules:
  0.0 96.7 jit_solution(8213067805707863018)
XLA Ops:
  0.6 94.8 %hyena_block.1 = (bf16[192,512]{1,0:T(8,128)(2,1)S(1)}, bf16[192,512]{1,0:T(8,128)(2,1)S(1)}, f32[3,128,512]{2,1,0:T(8,128)S(1)}, f32[32,128]{1,0:T(8,128)S(1)}, f32[3,3,512]{2,1,0:T(4,128)S(1)}) custom-call(bf16[192,512]{1,0:T(8,128)(2,1)} %refs_0_.1, bf16[3,128,512]{2,1,0:T(8,128)(2,1)} %bitcast.2, f32[3,3,512]{2,1,0:T(4,128)} %refs_2_.1, ...), custom_call_target="tpu_custom_call" | custom-call | tf_op jit(solution)/shard_map/hyena_block/pallas_call | solution.py:642
  95.4 1.1 %hand_over.1 = (bf16[192,512]{1,0:T(8,128)(2,1)}, bf16[192,512]{1,0:T(8,128)(2,1)}, f32[3,128,512]{2,1,0:T(8,128)}, f32[32,128]{1,0:T(8,128)}, f32[3,3,512]{2,1,0:T(4,128)}) custom-call(bf16[192,512]{1,0:T(8,128)(2,1)S(1)} %get-tuple-element.15.refs_0_, bf16[192,512]{1,0:T(8,128)(2,1)S(1)} %get-tuple-element.16.refs_1_, ...), custom_call_target="tpu_custom_call" | custom-call | tf_op jit(solution)/shard_map/hand_over/pallas_call | solution.py:668

commit v4 on v3

--- a/solution.py
+++ b/solution.py
@@ -9,41 +9,19 @@
 F32, BF16 = jnp.float32, jnp.bfloat16
 SIGNS = (1, -1)
 UNROLL = 1
-LINK_RATE = {"z": 46.0e3, "x": 46.0e3, "y": 46.0e3, "d": 600.0e3}
-LINK_LATENCY = {"z": 1.6, "x": 1.6, "y": 1.6, "d": 1.0}
-
-
-def planned_order(tasks, msgs):
-    arrival, done, link_free = {}, {}, {}
-    left, order, now = list(tasks), [], 0.0
-    while left:
-        best = None
-        for at, task in enumerate(left):
-            ready = 0.0
-            for dep in task["deps"]:
-                when = arrival.get(dep, done.get(dep))
-                if when is None:
-                    ready = None
-                    break
-                ready = max(ready, when)
-            if ready is None:
-                continue
-            key = (max(ready, now), task["prio"], ready, at)
-            if best is None or key < best[0]:
-                best = (key, at)
-        task = left.pop(best[1])
-        now = best[0][0] + task["cost"]
-        done[task["name"]] = now
-        order.append(task)
-        for name in task["sends"]:
-            link, nbytes, hops = msgs[name]["link"], msgs[name]["bytes"], msgs[name]["hops"]
-            arrival[name] = 0.0
-            for one in ("x+", "x-") if link == "x2" else (link,):
-                load = nbytes * (1 if link == "x2" else hops)
-                begin = max(now, link_free.get(one, 0.0))
-                link_free[one] = begin + load / LINK_RATE[one[0]]
-                arrival[name] = max(arrival[name], link_free[one] + LINK_LATENCY[one[0]] * hops)
-    return order, now
+
+ORDER = (
+    30, 2, 6, 0, 33, 67, 61, 64, 92, 110, 13, 9, 32, 40, 43, 50, 34, 38, 37, 35, 7, 47, 31, 3,
+    36, 78, 62, 81, 63, 71, 74, 14, 16, 19, 10, 44, 42, 41, 45, 39, 8, 23, 26, 4, 1, 66, 68, 69,
+    65, 54, 57, 48, 49, 52, 15, 17, 51, 85, 88, 80, 82, 79, 83, 46, 20, 11, 75, 76, 73, 72, 59, 56,
+    55, 58, 24, 53, 27, 5, 70, 60, 111, 18, 87, 86, 90, 89, 84, 21, 12, 77, 91, 28, 25, 93, 105, 107,
+    94, 22, 103, 95, 104, 29, 96, 101, 100, 102, 98, 106, 99, 108, 97, 109, 112, 113, 114, 115, 127, 125, 151, 130,
+    148, 131, 120, 141, 176, 144, 117, 119, 135, 129, 152, 149, 118, 133, 177, 142, 145, 189, 132, 128, 178, 218, 210, 150,
+    216, 153, 195, 193, 190, 231, 181, 143, 146, 137, 179, 233, 126, 182, 223, 155, 154, 162, 221, 185, 180, 205, 200, 203,
+    217, 219, 198, 147, 159, 166, 194, 139, 186, 228, 226, 134, 156, 116, 121, 174, 183, 220, 172, 163, 136, 196, 187, 157,
+    184, 199, 222, 204, 224, 160, 191, 188, 206, 229, 167, 227, 197, 164, 201, 138, 192, 232, 234, 140, 208, 225, 236, 158,
+    161, 173, 211, 122, 207, 124, 230, 237, 165, 168, 209, 239, 214, 202, 213, 175, 170, 235, 171, 169, 212, 123, 238, 215,
+)
 
 
 def block_kernel(
@@ -221,8 +199,8 @@
         flat = go[...].reshape(ntok, 128).T
         gox[:, :, 0:ntok] = flat.reshape(ngroups, members, ntok)
 
-    msg("goh", lambda: gox.at[:, :, pl.ds(0, 256)], lambda: gox.at[:, :, pl.ds(ntok, 256)], lambda: at_z(-1), "z-", 128 * 512)
-    task("got", deps=[("goq", 1), ("goq", 2), ("goq", 3)], run=turn_gout, sends=["goh"], cost=0.3, prio=3)
+    msg(("goh",), lambda: gox.at[:, :, pl.ds(0, 256)], lambda: gox.at[:, :, pl.ds(ntok, 256)], lambda: at_z(-1), "z-", 128 * 512)
+    task("got", deps=[("goq", 1), ("goq", 2), ("goq", 3)], run=turn_gout, sends=[("goh",)], cost=0.3, prio=3)
 
     def edge_rows():
         edge[0] = acc[0:144, :].astype(BF16)
@@ -251,7 +229,7 @@
         ahead = gox[:, :, ntok : ntok + 256]
         gox[:, :, ntok : ntok + 256] = jnp.where(z == nz - 1, jnp.zeros_like(ahead), ahead)
 
-    task("halo", deps=halos + ["goh", "mxt", "got"], run=turn_halos, cost=0.3, prio=0)
+    task("halo", deps=halos + [("goh",), "mxt", "got"], run=turn_halos, cost=0.3, prio=0)
 
     span = ntok + 128
 
@@ -377,18 +355,24 @@
 
     task("mixed_out", deps=[("mq", m) for m in (1, 2, 3)] + ["mixed_send"], run=mixed_final, cost=0.1, prio=9)
 
-    def weight_partial(e):
+    def weight_partial(e, far):
         zc = wrap(z + e, nz)
-        out = jnp.dot(gmt[...].reshape(384, ntok), tok[zc].reshape(ntok, cols), preferred_element_type=F32)
-        for n in range(4):
-            gp[e % nz, n] = out[:, n * 128 : (n + 1) * 128]
+        hf = 1 - xh if far else xh
+        rhs = tok[zc, :, :, pl.ds(pl.multiple_of(hf * 256, 256), 256)].reshape(ntok, 256)
+        out = jnp.dot(gmt[...].reshape(384, ntok), rhs, preferred_element_type=F32)
+        for n in range(2):
+            gp[e % nz, hf * 2 + n] = out[:, n * 128 : (n + 1) * 128]
 
     chunks = [half_z]
     for e in range(half_z - 1, 0, -1):
         chunks += [e, -e]
     chunks.append(0)
     for n, e in enumerate(chunks):
-        task(("gw", e % nz), deps=["local"], run=lambda e=e: weight_partial(e), cost=0.6, prio=3 + 0.05 * n)
+        for far in (True, False):
+            task(
+                ("gw", e % nz, far), deps=["local"], run=lambda e=e, far=far: weight_partial(e, far), cost=0.38,
+                prio=3 + 0.05 * n + (0 if far else 0.02),
+            )
     slot = {}
     for m in range(4):
         for d in SIGNS:
@@ -401,7 +385,7 @@
             for h in range(top, 0, -1):
                 s = slot[m, d, h]
                 name = msg(("wr", m, d, h), lambda s=s: ws.at[s], lambda s=s: wr.at[s], lambda d=d: at_z(d), "z+" if d > 0 else "z-", wbytes)
-                deps = [("gw", (d * h) % nz)]
+                deps = [("gw", (d * h) % nz, m >= 2)]
                 if h < top:
                     deps.append(("wr", m, d, h + 1))
                 elif m < 2:
@@ -423,7 +407,7 @@
             gw_out[i, :, lanes(mate(m))] = value[i * 128 : (i + 1) * 128, :].T
 
     for m in range(4):
-        deps = [("gw", 0), ("wr", m, 1, 1), ("wr", m, -1, 1)]
+        deps = [("gw", 0, m >= 2), ("wr", m, 1, 1), ("wr", m, -1, 1)]
         if m == 0:
             task("wtot0", deps=deps, run=lambda: weight_store(0, weight_total(0)), cost=0.5, prio=8)
             continue
@@ -533,6 +517,17 @@
             gin_out[h * 2 * quarter : (h + 1) * 2 * quarter, :] = total.astype(BF16)
 
         task(("gin", h), deps=[("s2h", h, 1), ("s2h", h, -1), ("s1", h, 0)], run=last, cost=0.1, prio=8)
+
+    sent = set()
+
+    def drain(kinds):
+        for name in msgs:
+            if name not in sent and name[0] in kinds:
+                copy_of(name).wait_send()
+                sent.add(name)
+
+    first_half = ("wq", "goq", "w", "t1", "t1q", "t2", "t2q", "td", "goh", "mh", "g")
+    task("drain1", deps=["mixed_out"], run=lambda: drain(first_half), cost=0.6, prio=9)
 
     barrier = pltpu.get_barrier_semaphore()
     peers = [at_z(e) for e in SIGNS] + [at_quad(m) for m in (1, 2, 3)] + [at_xy(a, d) for a in ("x", "y") for d in SIGNS]
@@ -557,7 +552,13 @@
     sfs[...] = jnp.zeros_like(sfs)
     pl.semaphore_wait(barrier, len(peers))
 
-    order, _ = planned_order(tasks, msgs)
+    assert sorted(ORDER) == list(range(len(tasks)))
+    order = [tasks[n] for n in ORDER]
+    finished, started_sends = set(), set()
+    for step in order:
+        assert all(dep in finished or dep in started_sends for dep in step["deps"])
+        finished.add(step["name"])
+        started_sends.update(step["sends"])
     waited = set()
     for step in order:
         for dep in step["deps"]:
@@ -569,7 +570,8 @@
         for name in step["sends"]:
             copy_of(name).start()
     for name in msgs:
-        copy_of(name).wait_send()
+        if name not in sent:
+            copy_of(name).wait_send()
 
 
 def scratch(nz, rows, cols, n_messages):

time: 98.5 us -> 96 us (0.975); the launches traced: 96.7 us -> 95.9 us
  no operation moved by 1% of the time
where the time goes in v4:
time: 96 us; the launch traced here: 95.9 us
  Pallas kernels  95.1 us (99%)
    pallas_call x1, Pallas kernels, per_device(): pl.pallas_call(body, out_shape=(pltpu.VMEM((rows, cols), BF16), pltpu.VME...  94.1 us

profile of v4, /device:TPU:1, one launch (start us, length us, event | category | flops | bytes accessed | tf_op | source)
XLA Modules:
  0.0 95.9 jit_solution(13230159946701868510)
XLA Ops:
  0.6 94.1 %hyena_block.1 = (bf16[192,512]{1,0:T(8,128)(2,1)S(1)}, bf16[192,512]{1,0:T(8,128)(2,1)S(1)}, f32[3,128,512]{2,1,0:T(8,128)S(1)}, f32[32,128]{1,0:T(8,128)S(1)}, f32[3,3,512]{2,1,0:T(4,128)S(1)}) custom-call(bf16[192,512]{1,0:T(8,128)(2,1)} %refs_0_.1, bf16[3,128,512]{2,1,0:T(8,128)(2,1)} %bitcast.2, f32[3,3,512]{2,1,0:T(4,128)} %refs_2_.1, ...), custom_call_target="tpu_custom_call" | custom-call | tf_op jit(solution)/shard_map/hyena_block/pallas_call | solution.py:644
  94.7 1.1 %hand_over.1 = (bf16[192,512]{1,0:T(8,128)(2,1)}, bf16[192,512]{1,0:T(8,128)(2,1)}, f32[3,128,512]{2,1,0:T(8,128)}, f32[32,128]{1,0:T(8,128)}, f32[3,3,512]{2,1,0:T(4,128)}) custom-call(bf16[192,512]{1,0:T(8,128)(2,1)S(1)} %get-tuple-element.15.refs_0_, bf16[192,512]{1,0:T(8,128)(2,1)S(1)} %get-tuple-element.16.refs_1_, ...), custom_call_target="tpu_custom_call" | custom-call | tf_op jit(solution)/shard_map/hand_over/pallas_call | solution.py:670

commit v5 on v4

--- a/solution.py
+++ b/solution.py
@@ -560,7 +560,12 @@
         finished.add(step["name"])
         started_sends.update(step["sends"])
     waited = set()
-    for step in order:
+    launched = []
+    for at, step in enumerate(order):
+        if at in (len(order) - 24, len(order) - 12):
+            for name in [n for n, begun in launched if begun < at - 24 and n not in sent]:
+                copy_of(name).wait_send()
+                sent.add(name)
         for dep in step["deps"]:
             if dep in msgs and dep not in waited:
                 copy_of(dep).wait_recv()
@@ -569,6 +574,7 @@
             step["run"]()
         for name in step["sends"]:
             copy_of(name).start()
+            launched.append((name, at))
     for name in msgs:
         if name not in sent:
             copy_of(name).wait_send()

time: 96 us -> 95.9 us (level)
  no operation moved by 1% of the time
where the time goes in v5:
time: 95.9 us; the launch traced here: 95.8 us
  Pallas kernels  95 us (99%)
    pallas_call x1, Pallas kernels, per_device(): pl.pallas_call(body, out_shape=(pltpu.VMEM((rows, cols), BF16), pltpu.VME...  93.9 us

profile of v5, /device:TPU:1, one launch (start us, length us, event | category | flops | bytes accessed | tf_op | source)
XLA Modules:
  0.0 95.8 jit_solution(4693195592059108489)
XLA Ops:
  0.6 93.9 %hyena_block.1 = (bf16[192,512]{1,0:T(8,128)(2,1)S(1)}, bf16[192,512]{1,0:T(8,128)(2,1)S(1)}, f32[3,128,512]{2,1,0:T(8,128)S(1)}, f32[32,128]{1,0:T(8,128)S(1)}, f32[3,3,512]{2,1,0:T(4,128)S(1)}) custom-call(bf16[192,512]{1,0:T(8,128)(2,1)} %refs_0_.1, bf16[3,128,512]{2,1,0:T(8,128)(2,1)} %bitcast.2, f32[3,3,512]{2,1,0:T(4,128)} %refs_2_.1, ...), custom_call_target="tpu_custom_call" | custom-call | tf_op jit(solution)/shard_map/hyena_block/pallas_call | solution.py:650
  94.6 1.1 %hand_over.1 = (bf16[192,512]{1,0:T(8,128)(2,1)}, bf16[192,512]{1,0:T(8,128)(2,1)}, f32[3,128,512]{2,1,0:T(8,128)}, f32[32,128]{1,0:T(8,128)}, f32[3,3,512]{2,1,0:T(4,128)}) custom-call(bf16[192,512]{1,0:T(8,128)(2,1)S(1)} %get-tuple-element.15.refs_0_, bf16[192,512]{1,0:T(8,128)(2,1)S(1)} %get-tuple-element.16.refs_1_, ...), custom_call_target="tpu_custom_call" | custom-call | tf_op jit(solution)/shard_map/hand_over/pallas_call | solution.py:676
